TPU v7x, 32 devices: a whole 2x2x4 slice. The times are simulated.
32 devices in a mesh: grp: 1, seq: 32 (over z, y, x, core), head: 1.
Axes of the slice: x: 2, y: 2, z: 4, core: 2. Of those that a mesh axis runs over, the one named last changes fastest.
Arguments:
- queries: bfloat16 [8192, 2048], P(('grp', 'seq'), 'head'), may hold values from -6 to 6
- keys: bfloat16 [8192, 2048], P(('grp', 'seq'), 'head'), may hold values from -6 to 6
- values: bfloat16 [8192, 2048], P(('grp', 'seq'), 'head'), may hold values from -6 to 6
- out_gain: float32 [2048], P('head'), may hold values from 0.4 to 1.6
- hash_ids: int32 [2, 128], replicated, may hold values from 0 to 15
- sign_ids: int32 [2, 128], replicated, may hold values from 0 to 1
Outputs:
- attended: bfloat16 [8192, 2048], P(('grp', 'seq'), 'head')
Inputs may be any that keep to these rules, and one draw needn't show every extreme that they name: `hash_ids`: bucket of feature i at each level. `sign_ids`: 1 stands for sign +1, 0 for -1.
All inputs are finite; a program needn't handle non-finite values.
Results may differ from a plain program's by a relative error of at most 0.0056.
Values may be sent and summed in bfloat16 or wider, within the bound.
No kernel may reach another device: no remote copies, remote signals or barrier semaphores. Data moves between devices by JAX's collectives and lax.ppermute only.
A program may use at most 64 MiB of HBM per device.

v0:
```python
import jax
import jax.numpy as jnp
from jax import lax
from jax.sharding import PartitionSpec as P

HD = 128
BUCKETS = 16


def from_behind(block, axis, distance):
    devices = range(lax.axis_size(axis))
    route = [(i - distance, i) for i in devices if i - distance in devices]
    return lax.ppermute(block, axis, route)


def sketch_matrix(hash_ids, sign_ids):
    buckets = jnp.arange(BUCKETS, dtype=jnp.int32)
    signs = (2 * sign_ids - 1).astype(jnp.float32)
    onehot = (hash_ids[:, :, None] == buckets[None, None, :]).astype(jnp.float32) * signs[
        :, :, None
    ]
    return jnp.concatenate([onehot[0], onehot[1]], axis=1).astype(jnp.bfloat16)


def head_features(rows, sketch):
    factor = 0.75 * (BUCKETS / HD) ** 0.5
    both = jnp.dot(rows, sketch, preferred_element_type=jnp.float32) * factor
    level = both[:, :BUCKETS] * both[:, BUCKETS:]
    outer = level[:, :, None] * level[:, None, :]
    return outer.reshape(rows.shape[0], BUCKETS * BUCKETS).astype(jnp.bfloat16)


def near_head(query_rows, key_rows, value_rows, key_before, value_before):
    block_rows = query_rows.shape[0]
    key_all = jnp.concatenate([key_before, key_rows], 0)
    value_all = jnp.concatenate([value_before, value_rows], 0)
    scores = jnp.einsum(
        "qd,kd->qk", query_rows, key_all, preferred_element_type=jnp.float32
    ) * float(HD) ** (-0.5)
    rows_index = jnp.arange(block_rows, dtype=jnp.int32)[:, None]
    cols_index = jnp.arange(2 * block_rows, dtype=jnp.int32)[None, :]
    allowed = cols_index <= rows_index + block_rows
    weights = jnp.where(allowed, scores**4, 0.0).astype(jnp.bfloat16)
    return jnp.dot(weights, value_all, preferred_element_type=jnp.float32)


def column(block, head_number):
    return lax.dynamic_slice_in_dim(block, head_number * HD, HD, 1)


def local(queries, keys, values, out_gain, hash_ids, sign_ids):
    block_rows = queries.shape[0]
    heads_here = queries.shape[1] // HD
    sketch = sketch_matrix(hash_ids, sign_ids)
    key_prev, value_prev = from_behind((keys, values), "seq", 1)
    head_list = jnp.arange(heads_here, dtype=jnp.int32)

    def block_state(key_block, value_block):

        def one_head(head_number):
            phi_key = head_features(column(key_block, head_number), sketch)
            return jnp.einsum(
                "tf,td->fd",
                phi_key,
                column(value_block, head_number),
                preferred_element_type=jnp.float32,
            )

        return lax.map(one_head, head_list)

    own_state = block_state(keys, values)
    previous = block_state(key_prev, value_prev)
    devices = lax.axis_size("seq")
    flat = own_state.reshape(devices, -1, HD)
    received = lax.all_to_all(flat, "seq", split_axis=0, concat_axis=0, tiled=True)
    running = jnp.cumsum(received, axis=0)
    leading = jnp.zeros((1,) + received.shape[1:], jnp.float32)
    exclusive = jnp.concatenate([leading, running[:-1]], axis=0)
    gathered = lax.all_to_all(exclusive, "seq", split_axis=0, concat_axis=0, tiled=True)
    earlier_sum = gathered.reshape(own_state.shape)
    far_state = earlier_sum - previous
    far_half = far_state.astype(jnp.bfloat16)
    gain_rows = out_gain.reshape(heads_here, HD)

    def attend(head_number):
        query_rows = column(queries, head_number)
        near_sum = near_head(
            query_rows,
            column(keys, head_number),
            column(values, head_number),
            column(key_prev, head_number),
            column(value_prev, head_number),
        )
        phi_query = head_features(query_rows, sketch)
        far_head = lax.dynamic_index_in_dim(far_half, head_number, 0, keepdims=False)
        distant = jnp.dot(phi_query, far_head, preferred_element_type=jnp.float32)
        mixed = near_sum + distant
        mean_square = jnp.mean(mixed * mixed, axis=-1, keepdims=True)
        gain_head = lax.dynamic_index_in_dim(gain_rows, head_number, 0, keepdims=False)
        return (mixed * lax.rsqrt(mean_square + 1e-06) * gain_head[None]).astype(jnp.bfloat16)

    results = lax.map(attend, head_list)
    return jnp.transpose(results, (1, 0, 2)).reshape(block_rows, heads_here * HD)


def solution(mesh):
    in_specs = (
        P(("grp", "seq"), "head"),
        P(("grp", "seq"), "head"),
        P(("grp", "seq"), "head"),
        P("head"),
        P(),
        P(),
    )
    out_specs = P(("grp", "seq"), "head")
    return jax.shard_map(local, mesh=mesh, in_specs=in_specs, out_specs=out_specs, check_vma=False)
```

profile of v0, /device:TPU:16, one launch (start us, length us, event | category | flops | bytes accessed | tf_op | source)
XLA Modules:
  0.0 383.5 jit_solution(10691543118928223271)
XLA Ops:
  1.7 55.2 %while.30 = (s32[]{:T(128)}, f32[16,256,128]{2,1,0:T(8,128)S(1)}, s32[16]{0:T(128)S(1)}, bf16[256,2048]{1,0:T(8,128)(2,1)}, bf16[128,32]{1,0:T(8,128)(2,1)S(1)},...) while((s32[]{:T(128)}, f32[16,256,128]{2,1,0:T(8,128)S(1)}, ...), condition=%wide.region_1.2_spmd, body=%wide.region_0.1_spmd.sunk | while | flops 19017732 | bytes 631463 | solution.py:69
  57.0 1.3 copy-done
  58.3 5.9 %all-to-all-start = ((f32[32,128,128]{2,1,0:T(8,128)}), f32[32,128,128]{2,1,0:T(8,128)S(1)}, u32[]{:S(2)}, u32[]{:S(2)}) async-start(f32[32,128,128]{2,1,0:T(8,128)} %bitcast.84), calls=%async_computation | async-start | bytes 4194304 | tf_op jit(solution)/shard_map/all_to_all | solution.py:75
  64.3 2.0 collective-permute-start
  66.3 3.4 collective-permute-start.1
  69.7 40.8 %all-to-all-done = f32[32,128,128]{2,1,0:T(8,128)S(1)} async-done(((f32[32,128,128]{2,1,0:T(8,128)}), f32[32,128,128]{2,1,0:T(8,128)S(1)}, u32[]{:S(2)}, u32[]{:S(2)}) %all-to-all-start) | async-done | bytes 2097184 | tf_op jit(solution)/shard_map/all_to_all | solution.py:75
  110.5 6.5 %fusion.44 = f32[32,128,128]{2,1,0:T(8,128)S(1)} fusion(f32[32,128,128]{2,1,0:T(8,128)S(1)} %all-to-all-done), kind=kOutput, calls=%fused_computation.68 | output fusion | flops 16252928 | bytes 4194304 | tf_op jit(solution)/shard_map/jit(cumsum)/reduce_window_sum | solution.py:76
  117.2 1.5 concatenate.14
  118.7 6.7 %all-to-all-start.1 = ((f32[32,128,128]{2,1,0:T(8,128)}), f32[32,128,128]{2,1,0:T(8,128)S(1)}, u32[]{:S(2)}, u32[]{:S(2)}) async-start(f32[32,128,128]{2,1,0:T(8,128)} %concatenate.14), calls=%async_computation.1 | async-start | bytes 4194304 | tf_op jit(solution)/shard_map/all_to_all | solution.py:79
  125.5 40.1 %collective-permute-done.1 = bf16[256,2048]{1,0:T(8,128)(2,1)} collective-permute-done((bf16[256,2048]{1,0:T(8,128)(2,1)}, bf16[256,2048]{1,0:T(8,128)(2,1)}, u32[]{:S(2)}, u32[]{:S(2)}) %collective-permute-start.1) | collective-permute-done | bytes 1048608 | tf_op jit(solution)/shard_map/ppermute | solution.py:13
  165.6 1.5 broadcast.70.clone
  167.1 65.4 %while.31 = (s32[]{:T(128)}, f32[16,256,128]{2,1,0:T(8,128)}, s32[16]{0:T(128)S(1)}, bf16[256,2048]{1,0:T(8,128)(2,1)}, bf16[128,32]{1,0:T(8,128)(2,1)S(1)}, /*i...) while((s32[]{:T(128)}, f32[16,256,128]{2,1,0:T(8,128)}, s32[16]{0:T(128)S(1)}, ...), condition=%wide.region_4.5_spmd, body=%wide.region_3.4_spmd.sunk | while | flops 19017732 | bytes 631463 | solution.py:69
  169.5 1.7 fusion.80
  172.6 1.0 convolution_multiply_fusion.8
  173.6 1.7 fusion.80
  177.7 1.7 fusion.80
  181.8 1.7 fusion.80
  185.9 1.7 fusion.80
  190.0 1.7 fusion.80
  194.0 1.7 fusion.80
  198.1 1.7 fusion.80
  202.2 1.7 fusion.80
  206.3 1.7 fusion.80
  210.4 1.7 fusion.80
  214.5 1.7 fusion.80
  218.6 1.7 fusion.80
  222.7 1.7 fusion.80
  226.7 1.7 fusion.80
  230.8 1.7 fusion.80
  232.5 1.8 fusion.43
  234.3 146.9 %while.32 = (s32[]{:T(128)}, bf16[16,256,128]{1,2,0:T(8,128)(2,1)}, s32[16]{0:T(128)S(1)}, bf16[256,2048]{1,0:T(8,128)(2,1)}, bf16[256,2048]{1,0:T(8,128)(2,1)},...) while((s32[]{:T(128)}, bf16[16,256,128]{1,2,0:T(8,128)(2,1)}, ...), condition=%wide.region_7.8_spmd, body=%wide.region_5.7_spmd.sunk | while | flops 87634440 | bytes 1949961 | solution.py:102
  237.5 1.2 fusion.87
  246.7 1.2 fusion.87
  255.8 1.3 fusion.87
  265.0 1.2 fusion.87
  274.2 1.3 fusion.87
  283.4 1.2 fusion.87
  292.6 1.2 fusion.87
  301.7 1.2 fusion.87
  310.9 1.2 fusion.87
  320.1 1.2 fusion.87
  329.3 1.3 fusion.87
  338.5 1.2 fusion.87
  347.7 1.2 fusion.87
  356.8 1.2 fusion.87
  366.0 1.2 fusion.87
  375.2 1.2 fusion.87
  381.2 2.3 copy.19
  (333 shorter events, 153.6 us)
Async XLA Ops:
  57.0 1.3 copy-start
  58.3 52.2 %all-to-all-start = ((f32[32,128,128]{2,1,0:T(8,128)}), f32[32,128,128]{2,1,0:T(8,128)S(1)}, u32[]{:S(2)}, u32[]{:S(2)}) async-start(f32[32,128,128]{2,1,0:T(8,128)} %bitcast.84), calls=%async_computation | async-start | bytes 4194304 | tf_op jit(solution)/shard_map/all_to_all | solution.py:75
  64.3 61.2 %collective-permute-start = (bf16[256,2048]{1,0:T(8,128)(2,1)}, bf16[256,2048]{1,0:T(8,128)(2,1)}, u32[]{:S(2)}, u32[]{:S(2)}) collective-permute-start(bf16[256,2048]{1,0:T(8,128)(2,1)} %param.13), channel_id=1, source_target_pairs={{0,1},{1,2},{2,3},{3,4},{4,5},{5,6},{6,7},{7,8},{8,9},{9,10},{10,1... | collective-permute-start | bytes 3145736 | tf_op jit(solution)/shard_map/ppermute | solution.py:13
  66.3 99.3 %collective-permute-start.1 = (bf16[256,2048]{1,0:T(8,128)(2,1)}, bf16[256,2048]{1,0:T(8,128)(2,1)}, u32[]{:S(2)}, u32[]{:S(2)}) collective-permute-start(bf16[256,2048]{1,0:T(8,128)(2,1)} %param.14), channel_id=1, source_target_pairs={{0,1},{1,2},{2,3},{3,4},{4,5},{5,6},{6,7},{7,8},{8,9},{9,10},{10,1... | collective-permute-start | bytes 3145736 | tf_op jit(solution)/shard_map/ppermute | solution.py:13
  118.7 113.8 %all-to-all-start.1 = ((f32[32,128,128]{2,1,0:T(8,128)}), f32[32,128,128]{2,1,0:T(8,128)S(1)}, u32[]{:S(2)}, u32[]{:S(2)}) async-start(f32[32,128,128]{2,1,0:T(8,128)} %concatenate.14), calls=%async_computation.1 | async-start | bytes 4194304 | tf_op jit(solution)/shard_map/all_to_all | solution.py:79
where the time goes:
time: 391 us; the launch traced here: 384 us
  matrix products  116 us (30%)
  waiting for transfers between devices  81 us (21%)
  local copies, waits for them, and re-layouts  78 us (20%)
  loops' own time  68 us (17%)
  other arithmetic  22.5 us (6%)
  starting transfers between devices  18.1 us (5%)
    dot_general x48, matrix products, head_features(): both = jnp.dot(rows, sketch, preferred_element_type=jnp.float32) * factor  49.1 us
    another operation x1, loops' own time, local(): results = lax.map(attend, head_list)  44.7 us
    dot_general x32, matrix products, one_head(): jnp.einsum('tf,td->fd', phi_key, column(value_block, head_number), prefer...  43 us
    all_to_all x1, waiting for transfers between devices, local(): lax.all_to_all(flat, 'seq', split_axis=0, concat_axis=0, tiled=True)  40.8 us
    ppermute x2, waiting for transfers between devices, from_behind(): return lax.ppermute(block, axis, route)  40.1 us
    dynamic_slice x48, local copies, waits for them, and re-layouts, block_state(): return lax.map(one_head, head_list)  31.3 us
    dynamic_slice x32, local copies, waits for them, and re-layouts, column(): return lax.dynamic_slice_in_dim(block, head_number * HD, HD, 1)  28.5 us
    another operation x2, loops' own time, block_state(): return lax.map(one_head, head_list)  23.3 us
  transfers between devices with their start and end apart: 4, of which 2 were waited for; matrix products, arithmetic and copies ran while one was open for 17% of the time, Pallas kernels for 0%

commit v1 on v0

v1 whole, which is shorter than its diff:
```python
import jax
import jax.numpy as jnp
from jax import lax
from jax.experimental import pallas as pl
from jax.experimental.pallas import tpu as pltpu
from jax.sharding import PartitionSpec as P

HD = 128
BUCKETS = 16
SHIFTS = BUCKETS // 2 + 1
FEATURES = SHIFTS * BUCKETS
FACTOR4 = (0.75 * (BUCKETS / HD) ** 0.5) ** 4
EPS = 1e-06
BF16 = jnp.bfloat16
F32 = jnp.float32


def dot_nt(a, b):
    return lax.dot_general(a, b, (((1,), (1,)), ((), ())), preferred_element_type=F32)


def dot_nn(a, b):
    return lax.dot_general(a, b, (((1,), (0,)), ((), ())), preferred_element_type=F32)


def sketch_rows(buckets, hash_row, sign_row, weight=1.0):
    signs = (2 * sign_row - 1).astype(F32) * weight
    return jnp.where(hash_row == buckets, signs, 0.0).astype(BF16)


def head_cols(head):
    return pl.ds(head * HD, HD)


def state_kernel(hash_ref, sign_ref, key_ref, value_ref, total_ref):
    heads = key_ref.shape[1] // HD
    row = lax.broadcasted_iota(jnp.int32, (FEATURES, HD), 0)
    buckets = (row + row // BUCKETS) % BUCKETS
    sketch = jnp.concatenate(
        [
            sketch_rows(buckets, hash_ref[level : level + 1, :], sign_ref[level : level + 1, :])
            for level in range(2)
        ],
        0,
    )
    for head in range(heads):
        both = dot_nt(sketch, key_ref[:, head_cols(head)])
        level = both[:FEATURES] * both[FEATURES:]
        base = level[:BUCKETS] * FACTOR4
        phi = jnp.concatenate(
            [base * level[d * BUCKETS : (d + 1) * BUCKETS] for d in range(SHIFTS)], 0
        ).astype(BF16)
        total = dot_nn(phi, value_ref[:, head_cols(head)])
        total_ref[head] = total.astype(total_ref.dtype)


def quartic(scores):
    squared = scores * scores * (1.0 / HD)
    return squared * squared


def own_kernel(query_ref, key_ref, value_ref, near_ref):
    rows = query_ref.shape[0]
    heads = query_ref.shape[1] // HD
    half = rows // 2
    rows_index = lax.broadcasted_iota(jnp.int32, (half, half), 0)
    cols_index = lax.broadcasted_iota(jnp.int32, (half, half), 1)
    allowed = cols_index <= rows_index
    for head in range(heads):
        cols = head_cols(head)
        key_top, key_low = key_ref[:half, cols], key_ref[half:, cols]
        value_top, value_low = value_ref[:half, cols], value_ref[half:, cols]
        top = jnp.where(allowed, quartic(dot_nt(query_ref[:half, cols], key_top)), 0.0)
        near_ref[:half, cols] = dot_nn(top.astype(BF16), value_top)
        query_low = query_ref[half:, cols]
        left = quartic(dot_nt(query_low, key_top))
        right = jnp.where(allowed, quartic(dot_nt(query_low, key_low)), 0.0)
        near_ref[half:, cols] = dot_nn(left.astype(BF16), value_top) + dot_nn(
            right.astype(BF16), value_low
        )


def before_kernel(query_ref, key_ref, value_ref, own_ref, near_ref):
    heads = query_ref.shape[1] // HD
    for head in range(heads):
        cols = head_cols(head)
        weights = quartic(dot_nt(query_ref[:, cols], key_ref[:, cols])).astype(BF16)
        near_ref[:, cols] = own_ref[:, cols] + dot_nn(weights, value_ref[:, cols])


def far_kernel(hash_ref, sign_ref, query_ref, far_ref, near_ref, gain_ref, out_ref):
    heads = query_ref.shape[1] // HD
    row = lax.broadcasted_iota(jnp.int32, (HD, HD), 0)
    base_bucket = row % BUCKETS
    shift = row // BUCKETS
    weight = jnp.where(shift == 0, 1.0, 2.0)
    pieces = []
    for level in range(2):
        hash_row = hash_ref[level : level + 1, :]
        sign_row = sign_ref[level : level + 1, :]
        pieces.append(sketch_rows(base_bucket, hash_row, sign_row))
        pieces.append(
            sketch_rows(
                (base_bucket + shift) % BUCKETS, hash_row, sign_row, weight if level == 0 else 1.0
            )
        )
    sketch = jnp.concatenate(pieces, 0)
    for head in range(heads):
        cols = head_cols(head)
        both = dot_nt(query_ref[:, cols], sketch)
        first = both[:, :HD] * both[:, 2 * HD : 3 * HD] * FACTOR4
        second = both[:, HD : 2 * HD] * both[:, 3 * HD :]
        opposite = second[:, :BUCKETS]
        opposite = jnp.concatenate(
            [opposite[:, BUCKETS // 2 :], opposite[:, : BUCKETS // 2]], 1
        )
        last = first[:, :BUCKETS] * opposite
        phi = jnp.concatenate([(first * second).astype(BF16), last.astype(BF16)], 1)
        mixed = near_ref[:, cols] + dot_nn(phi, far_ref[head])
        mean_square = jnp.mean(mixed * mixed, axis=-1, keepdims=True)
        out_ref[:, cols] = (
            mixed * lax.rsqrt(mean_square + EPS) * gain_ref[:, cols]
        ).astype(BF16)


def kernel_call(body, out_shape, *args):
    return pl.pallas_call(
        body,
        out_shape=out_shape,
        compiler_params=pltpu.CompilerParams(vmem_limit_bytes=48 * 1024 * 1024),
        name=body.__name__,
    )(*args)


def from_behind(block, axis, distance):
    devices = range(lax.axis_size(axis))
    route = [(i - distance, i) for i in devices if i - distance in devices]
    return lax.ppermute(block, axis, route)


def local(queries, keys, values, out_gain, hash_ids, sign_ids):
    rows, width = queries.shape
    heads = width // HD
    devices = lax.axis_size("seq")
    near_shape = jax.ShapeDtypeStruct((rows, width), F32)
    state_shape = jax.ShapeDtypeStruct((heads, FEATURES, HD), BF16)

    key_prev, value_prev = from_behind((keys, values), "seq", 1)
    total = kernel_call(state_kernel, state_shape, hash_ids, sign_ids, keys, values)
    flat = total.reshape(devices, -1, HD)
    received = lax.all_to_all(flat, "seq", split_axis=0, concat_axis=0, tiled=True)
    running = jnp.cumsum(received.astype(F32), axis=0)
    exclusive = jnp.concatenate(
        [jnp.zeros((2,) + running.shape[1:], F32), running[:-2]], axis=0
    ).astype(BF16)
    gathered = lax.all_to_all(exclusive, "seq", split_axis=0, concat_axis=0, tiled=True)
    far = gathered.reshape(heads, FEATURES, HD)

    near = kernel_call(own_kernel, near_shape, queries, keys, values)
    near = kernel_call(before_kernel, near_shape, queries, key_prev, value_prev, near)
    return kernel_call(
        far_kernel,
        jax.ShapeDtypeStruct((rows, width), BF16),
        hash_ids,
        sign_ids,
        queries,
        far,
        near,
        out_gain.reshape(1, width),
    )


def solution(mesh):
    in_specs = (
        P(("grp", "seq"), "head"),
        P(("grp", "seq"), "head"),
        P(("grp", "seq"), "head"),
        P("head"),
        P(),
        P(),
    )
    out_specs = P(("grp", "seq"), "head")
    return jax.shard_map(local, mesh=mesh, in_specs=in_specs, out_specs=out_specs, check_vma=False)
```

time: 391 us -> 82.7 us (0.21); the launches traced: 384 us -> 82.3 us
  matrix products: 116 us -> 0 us
  local copies, waits for them, and re-layouts: 78 us -> 6.06 us
  loops' own time: 68 us -> 0 us
  waiting for transfers between devices: 81 us -> 28 us
  other arithmetic: 22.5 us -> 0.13 us
  blocking collectives: 0 us -> 20.3 us
  Pallas kernels: 0 us -> 16.6 us
  starting transfers between devices: 18.1 us -> 11 us
    dot_general x112 -> x0, matrix products: 116 us -> none  [the longest x48 49.1 us: head_features(): both = jnp.dot(rows, sketch, preferred_element_type=jnp.float32) * factor]
    another operation x3 -> x0, loops' own time: 68 us -> none  [the longest x1 44.7 us: local(): results = lax.map(attend, head_list)]
    dynamic_slice x80 -> x0, local copies, waits for them, and re-layouts: 59.7 us -> none  [the longest x48 31.3 us: block_state(): return lax.map(one_head, head_list)]
    all_to_all x1 -> x0, waiting for transfers between devices: 40.8 us -> none  [local(): lax.all_to_all(flat, 'seq', split_axis=0, concat_axis=0, tiled=True)]
    all_to_all x0 -> x1, blocking collectives: none -> 20.3 us  [local(): lax.all_to_all(flat, 'seq', split_axis=0, concat_axis=0, tiled=True)]
    pallas_call x0 -> x4, Pallas kernels: none -> 16.6 us  [kernel_call(): pl.pallas_call(body, out_shape=out_shape, compiler_params=pltpu.CompilerP...]
    ppermute x2, waiting for transfers between devices: 40.1 us -> 28 us  [from_behind(): return lax.ppermute(block, axis, route)]
    dynamic_update_slice x16 -> x0, other arithmetic: 11.5 us -> none  [local(): results = lax.map(attend, head_list)]
  transfers between devices with their start and end apart: 4 -> 3, of which waited for: 2 -> 2; matrix products, arithmetic and copies ran while one was open for 17% -> 0% of each run, Pallas kernels for 0% -> 8%
where the time goes in v1:
time: 82.7 us; the launch traced here: 82.3 us
  waiting for transfers between devices  28 us (34%)
  blocking collectives  20.3 us (25%)
  Pallas kernels  16.6 us (20%)
  starting transfers between devices  11 us (13%)
  local copies, waits for them, and re-layouts  6.06 us (7%)
    ppermute x2, waiting for transfers between devices, from_behind(): return lax.ppermute(block, axis, route)  28 us
    all_to_all x1, blocking collectives, local(): lax.all_to_all(flat, 'seq', split_axis=0, concat_axis=0, tiled=True)  20.3 us
    pallas_call x4, Pallas kernels, kernel_call(): pl.pallas_call(body, out_shape=out_shape, compiler_params=pltpu.CompilerP...  16.6 us
    all_to_all x1, starting transfers between devices, local(): lax.all_to_all(exclusive, 'seq', split_axis=0, concat_axis=0, tiled=True)  5.6 us
    ppermute x2, starting transfers between devices, from_behind(): return lax.ppermute(block, axis, route)  5.41 us
    unnamed x22, local copies, waits for them, and re-layouts  5.16 us
  transfers between devices with their start and end apart: 3, of which 2 were waited for; matrix products, arithmetic and copies ran while one was open for 0% of the time, Pallas kernels for 8%

profile of v1, /device:TPU:16, one launch (start us, length us, event | category | flops | bytes accessed | tf_op | source)
XLA Modules:
  0.0 82.3 jit_solution(2059165062944215341)
XLA Ops:
  0.0 0.0 copy-start.2
  0.0 1.2 %copy-done.2 = bf16[256,2048]{1,0:T(8,128)(2,1)S(1)} copy-done((bf16[256,2048]{1,0:T(8,128)(2,1)S(1)}, bf16[256,2048]{1,0:T(8,128)(2,1)}, u32[]{:S(2)}) %copy-start.2) | copy-done | bytes 1048600
  1.2 0.0 copy-start.4
  1.2 1.2 %copy-done.4 = bf16[256,2048]{1,0:T(8,128)(2,1)S(1)} copy-done((bf16[256,2048]{1,0:T(8,128)(2,1)S(1)}, bf16[256,2048]{1,0:T(8,128)(2,1)}, u32[]{:S(2)}) %copy-start.4) | copy-done | bytes 1048600
  2.5 0.0 copy-start.7
  2.5 0.7 copy-done.7
  3.1 0.0 copy-start.9
  3.1 0.7 copy-done.9
  3.8 3.2 %state_kernel.1 = bf16[16,144,128]{2,1,0:T(8,128)(2,1)S(1)} custom-call(s32[2,128]{1,0:T(2,128)S(1)} %copy-done.7, s32[2,128]{1,0:T(2,128)S(1)} %copy-done.9, bf16[256,2048]{1,0:T(8,128)(2,1)S(1)} %copy-done.2, bf16[256,2048]{1,0:T(8,128)(2,1)S(1)} %copy-done.4), custom_call_target="tpu_custom_call" | custom-call | tf_op jit(solution)/shard_map/state_kernel/pallas_call | solution.py:127
  7.0 20.3 %all_to_all.10 = bf16[32,72,128]{2,1,0:T(8,128)(2,1)S(1)} all-to-all(bf16[32,72,128]{2,1,0:T(8,128)(2,1)S(1)} %bitcast.3), channel_id=1, replica_groups=mesh['grp'=1,'seq'=32,'head'=1] {'seq'}, dimensions={0} | all-to-all | bytes 1179648 | tf_op jit(solution)/shard_map/all_to_all | solution.py:151
  27.3 0.0 copy-start.3
  27.3 0.0 copy-start.5
  27.4 0.0 copy-start
  27.4 0.1 fusion
  27.5 0.9 %concatenate.3 = bf16[32,72,128]{2,1,0:T(8,128)(2,1)} pad(bf16[30,72,128]{2,1,0:T(8,128)(2,1)S(1)} %slice.7, bf16[]{:T(256)} %constant.6.clone.1), padding=2_0x0_0x0_0 | pad | bytes 1142786 | tf_op jit(solution)/shard_map/concatenate | solution.py:153
  28.4 5.6 %all-to-all-start.1 = ((bf16[32,72,128]{2,1,0:T(8,128)(2,1)}), bf16[32,72,128]{2,1,0:T(8,128)(2,1)}, u32[]{:S(2)}, u32[]{:S(2)}) async-start(bf16[32,72,128]{2,1,0:T(8,128)(2,1)} %concatenate.3), calls=%async_computation.1 | async-start | bytes 1179648 | tf_op jit(solution)/shard_map/all_to_all | solution.py:156
  34.0 0.0 copy-done.3
  34.0 2.0 %collective-permute-start = (bf16[256,2048]{1,0:T(8,128)(2,1)S(1)}, bf16[256,2048]{1,0:T(8,128)(2,1)S(1)}, u32[]{:S(2)}, u32[]{:S(2)}) collective-permute-start(bf16[256,2048]{1,0:T(8,128)(2,1)S(1)} %copy-done.3), channel_id=1, source_target_pairs={{0,1},{1,2},{2,3},{3,4},{4,5},{5,6},{6,7},{7,8},{8,9},{9,10},{10,1... | collective-permute-start | bytes 3145736 | tf_op jit(solution)/shard_map/ppermute | solution.py:138
  36.0 0.0 copy-done.5
  36.1 3.4 %collective-permute-start.1 = (bf16[256,2048]{1,0:T(8,128)(2,1)S(1)}, bf16[256,2048]{1,0:T(8,128)(2,1)S(1)}, u32[]{:S(2)}, u32[]{:S(2)}) collective-permute-start(bf16[256,2048]{1,0:T(8,128)(2,1)S(1)} %copy-done.5), channel_id=1, source_target_pairs={{0,1},{1,2},{2,3},{3,4},{4,5},{5,6},{6,7},{7,8},{8,9},{9,10},{10,1... | collective-permute-start | bytes 3145736 | tf_op jit(solution)/shard_map/ppermute | solution.py:138
  39.4 0.0 copy-done
  39.5 3.6 %own_kernel.1.own_ref = f32[256,2048]{1,0:T(8,128)S(1)} custom-call(bf16[256,2048]{1,0:T(8,128)(2,1)S(1)} %copy-done, bf16[256,2048]{1,0:T(8,128)(2,1)S(1)} %copy-done.3, bf16[256,2048]{1,0:T(8,128)(2,1)S(1)} %copy-done.5), custom_call_target="tpu_custom_call" | custom-call | tf_op jit(solution)/shard_map/own_kernel/pallas_call | solution.py:127
  43.0 0.0 copy-start.1
  43.0 1.3 %copy-done.1 = f32[256,2048]{1,0:T(8,128)} copy-done((f32[256,2048]{1,0:T(8,128)}, f32[256,2048]{1,0:T(8,128)S(1)}, u32[]{:S(2)}) %copy-start.1) | copy-done | bytes 2097176
  44.4 0.0 copy-start.6
  44.4 0.0 copy-start.8
  44.4 0.0 copy-start.10
  44.4 16.8 %collective-permute-done.key_ref = bf16[256,2048]{1,0:T(8,128)(2,1)S(1)} collective-permute-done((bf16[256,2048]{1,0:T(8,128)(2,1)S(1)}, bf16[256,2048]{1,0:T(8,128)(2,1)S(1)}, u32[]{:S(2)}, u32[]{:S(2)}) %collective-permute-start) | collective-permute-done | bytes 1048608 | tf_op jit(solution)/shard_map/ppermute | solution.py:138
  61.2 11.2 %collective-permute-done.1.value_ref = bf16[256,2048]{1,0:T(8,128)(2,1)S(1)} collective-permute-done((bf16[256,2048]{1,0:T(8,128)(2,1)S(1)}, bf16[256,2048]{1,0:T(8,128)(2,1)S(1)}, u32[]{:S(2)}, u32[]{:S(2)}) %collective-permute-start.1) | collective-permute-done | bytes 1048608 | tf_op jit(solution)/shard_map/ppermute | solution.py:138
  72.4 3.1 %before_kernel.1.near_ref = f32[256,2048]{1,0:T(8,128)S(1)} custom-call(bf16[256,2048]{1,0:T(8,128)(2,1)S(1)} %copy-done, bf16[256,2048]{1,0:T(8,128)(2,1)S(1)} %collective-permute-done.key_ref, bf16[256,2048]{1,0:T(8,128)(2,1)S(1)} %collective-permute-done.1.value_ref, f32[256,2048]{1,0:T(8,128)} %copy-done.1), custom_call_target="tpu_custom_call" | custom-call | tf_op jit(solution)/shard_map/before_kernel/pallas_call | solution.py:127
  75.5 0.0 all-to-all-done.1
  75.5 0.0 copy-done.6
  75.5 0.0 copy-done.8
  75.5 0.0 copy-done.10
  75.5 6.8 %far_kernel.1 = bf16[256,2048]{1,0:T(8,128)(2,1)} custom-call(s32[2,128]{1,0:T(2,128)S(1)} %copy-done.8, s32[2,128]{1,0:T(2,128)S(1)} %copy-done.10, bf16[256,2048]{1,0:T(8,128)(2,1)S(1)} %copy-done, bf16[16,144,128]{2,1,0:T(8,128)(2,1)} %bitcast.1.far_ref, f32[256,2048]{1,0:T(8,128)S(1)} %before_kernel.1.near_ref, f32[1,2048]{1,0:T(1,128)S(1)} %bitcast.4), custom_call_target="tpu_custom_call" | custom-call | tf_op jit(solution)/shard_map/far_kernel/pallas_call | solution.py:127
  (1 shorter events, 0.0 us)
Async XLA Ops:
  0.0 1.2 %copy-start.2 = (bf16[256,2048]{1,0:T(8,128)(2,1)S(1)}, bf16[256,2048]{1,0:T(8,128)(2,1)}, u32[]{:S(2)}) copy-start(bf16[256,2048]{1,0:T(8,128)(2,1)} %key_ref.3) | copy-start | bytes 3145732
  1.2 1.2 %copy-start.4 = (bf16[256,2048]{1,0:T(8,128)(2,1)S(1)}, bf16[256,2048]{1,0:T(8,128)(2,1)}, u32[]{:S(2)}) copy-start(bf16[256,2048]{1,0:T(8,128)(2,1)} %value_ref.3) | copy-start | bytes 3145732
  2.5 0.7 copy-start.7
  3.1 0.7 copy-start.9
  27.3 6.7 %copy-start.3 = (bf16[256,2048]{1,0:T(8,128)(2,1)S(1)}, bf16[256,2048]{1,0:T(8,128)(2,1)}, u32[]{:S(2)}) copy-start(bf16[256,2048]{1,0:T(8,128)(2,1)} %key_ref.3) | copy-start | bytes 3145732
  27.3 8.7 %copy-start.5 = (bf16[256,2048]{1,0:T(8,128)(2,1)S(1)}, bf16[256,2048]{1,0:T(8,128)(2,1)}, u32[]{:S(2)}) copy-start(bf16[256,2048]{1,0:T(8,128)(2,1)} %value_ref.3) | copy-start | bytes 3145732
  27.4 12.1 %copy-start = (bf16[256,2048]{1,0:T(8,128)(2,1)S(1)}, bf16[256,2048]{1,0:T(8,128)(2,1)}, u32[]{:S(2)}) copy-start(bf16[256,2048]{1,0:T(8,128)(2,1)} %query_ref.5) | copy-start | bytes 3145732
  28.4 47.1 %all-to-all-start.1 = ((bf16[32,72,128]{2,1,0:T(8,128)(2,1)}), bf16[32,72,128]{2,1,0:T(8,128)(2,1)}, u32[]{:S(2)}, u32[]{:S(2)}) async-start(bf16[32,72,128]{2,1,0:T(8,128)(2,1)} %concatenate.3), calls=%async_computation.1 | async-start | bytes 1179648 | tf_op jit(solution)/shard_map/all_to_all | solution.py:156
  34.0 27.2 %collective-permute-start = (bf16[256,2048]{1,0:T(8,128)(2,1)S(1)}, bf16[256,2048]{1,0:T(8,128)(2,1)S(1)}, u32[]{:S(2)}, u32[]{:S(2)}) collective-permute-start(bf16[256,2048]{1,0:T(8,128)(2,1)S(1)} %copy-done.3), channel_id=1, source_target_pairs={{0,1},{1,2},{2,3},{3,4},{4,5},{5,6},{6,7},{7,8},{8,9},{9,10},{10,1... | collective-permute-start | bytes 3145736 | tf_op jit(solution)/shard_map/ppermute | solution.py:138
  36.1 36.3 %collective-permute-start.1 = (bf16[256,2048]{1,0:T(8,128)(2,1)S(1)}, bf16[256,2048]{1,0:T(8,128)(2,1)S(1)}, u32[]{:S(2)}, u32[]{:S(2)}) collective-permute-start(bf16[256,2048]{1,0:T(8,128)(2,1)S(1)} %copy-done.5), channel_id=1, source_target_pairs={{0,1},{1,2},{2,3},{3,4},{4,5},{5,6},{6,7},{7,8},{8,9},{9,10},{10,1... | collective-permute-start | bytes 3145736 | tf_op jit(solution)/shard_map/ppermute | solution.py:138
  43.0 1.3 %copy-start.1 = (f32[256,2048]{1,0:T(8,128)}, f32[256,2048]{1,0:T(8,128)S(1)}, u32[]{:S(2)}) copy-start(f32[256,2048]{1,0:T(8,128)S(1)} %own_kernel.1.own_ref) | copy-start | bytes 6291460
  44.4 31.1 %copy-start.6 = (f32[2048]{0:T(1024)S(1)}, f32[2048]{0:T(1024)}, u32[]{:S(2)}) copy-start(f32[2048]{0:T(1024)} %param.9) | copy-start | bytes 24580
  44.4 31.2 %copy-start.8 = (s32[2,128]{1,0:T(2,128)S(1)}, s32[2,128]{1,0:T(2,128)}, u32[]{:S(2)}) copy-start(s32[2,128]{1,0:T(2,128)} %hash_ref.3) | copy-start | bytes 3076
  44.4 31.2 %copy-start.10 = (s32[2,128]{1,0:T(2,128)S(1)}, s32[2,128]{1,0:T(2,128)}, u32[]{:S(2)}) copy-start(s32[2,128]{1,0:T(2,128)} %sign_ref.3) | copy-start | bytes 3076

commit v2 on v1

v2 whole, which is shorter than its diff:
```python
import jax
import jax.numpy as jnp
from jax import lax
from jax.experimental import pallas as pl
from jax.experimental.pallas import tpu as pltpu
from jax.sharding import PartitionSpec as P


HD = 128
BUCKETS = 16
SHIFTS = BUCKETS // 2 + 1
FEATURES = SHIFTS * BUCKETS
FACTOR4 = (0.75 * (BUCKETS / HD) ** 0.5) ** 4
FACTOR2 = (0.75 * (BUCKETS / HD) ** 0.5) ** 2
EPS = 1e-06
CORES = 2
PLANE = 4
BF16 = jnp.bfloat16
F32 = jnp.float32


def dot_nt(a, b):
    return lax.dot_general(a, b, (((1,), (1,)), ((), ())), preferred_element_type=F32)


def dot_nn(a, b):
    return lax.dot_general(a, b, (((1,), (0,)), ((), ())), preferred_element_type=F32)


def sketch_rows(buckets, hash_row, sign_row, weight=1.0):
    signs = (2 * sign_row - 1).astype(F32) * weight
    return jnp.where(hash_row == buckets, signs, 0.0).astype(BF16)


def head_cols(head):
    return pl.ds(head * HD, HD)


def place():
    index = lax.axis_index("seq")
    return index % CORES, (index // CORES) % PLANE


def head_of(core, quarter, inner, per_piece):
    return (core * PLANE + quarter) * per_piece + inner


def cols_of(head):
    return pl.ds(pl.multiple_of(head * HD, HD), HD)


def state_kernel(hash_ref, sign_ref, key_ref, value_ref, keep_ref, send_ref):
    core, chip = place()
    per_piece = keep_ref.shape[1]
    row = lax.broadcasted_iota(jnp.int32, (FEATURES, HD), 0)
    buckets = (row + row // BUCKETS) % BUCKETS
    sketch = jnp.concatenate(
        [
            sketch_rows(buckets, hash_ref[level : level + 1, :], sign_ref[level : level + 1, :])
            for level in range(2)
        ],
        0,
    )
    for side, total_ref in ((1 - core, send_ref), (core, keep_ref)):
        for piece in range(PLANE):
            for inner in range(per_piece):
                cols = cols_of(head_of(side, chip ^ piece, inner, per_piece))
                both = dot_nt(sketch, key_ref[:, cols])
                level = both[:FEATURES] * both[FEATURES:]
                base = level[:BUCKETS] * FACTOR4
                phi = jnp.concatenate(
                    [base * level[d * BUCKETS : (d + 1) * BUCKETS] for d in range(SHIFTS)], 0
                ).astype(BF16)
                total_ref[piece, inner] = dot_nn(phi, value_ref[:, cols])


def quartic(scores):
    squared = scores * scores * (1.0 / HD)
    return squared * squared


def own_kernel(query_ref, key_ref, value_ref, near_ref):
    rows = query_ref.shape[0]
    heads = query_ref.shape[1] // HD
    half = rows // 2
    rows_index = lax.broadcasted_iota(jnp.int32, (half, half), 0)
    cols_index = lax.broadcasted_iota(jnp.int32, (half, half), 1)
    allowed = cols_index <= rows_index
    for head in range(heads):
        cols = head_cols(head)
        key_top, key_low = key_ref[:half, cols], key_ref[half:, cols]
        value_top, value_low = value_ref[:half, cols], value_ref[half:, cols]
        top = jnp.where(allowed, quartic(dot_nt(query_ref[:half, cols], key_top)), 0.0)
        near_ref[:half, cols] = dot_nn(top.astype(BF16), value_top)
        query_low = query_ref[half:, cols]
        left = quartic(dot_nt(query_low, key_top))
        right = jnp.where(allowed, quartic(dot_nt(query_low, key_low)), 0.0)
        near_ref[half:, cols] = dot_nn(left.astype(BF16), value_top) + dot_nn(
            right.astype(BF16), value_low
        )


def split(x):
    high = x.astype(BF16)
    low = (x - high.astype(F32)).astype(BF16)
    return high, low


def before_kernel(hash_ref, sign_ref, query_ref, key_ref, value_ref, own_ref, near_ref):
    core, _ = place()
    even = jnp.where(core == 0, 1.0, 0.0)
    heads = query_ref.shape[1] // HD
    row = lax.broadcasted_iota(jnp.int32, (BUCKETS, HD), 0)
    sketch = jnp.concatenate(
        [
            sketch_rows(row, hash_ref[level : level + 1, :], sign_ref[level : level + 1, :])
            for level in range(2)
        ],
        0,
    )
    for head in range(heads):
        cols = head_cols(head)
        query, key = query_ref[:, cols], key_ref[:, cols]
        query_both = dot_nt(sketch, query)
        key_both = dot_nt(sketch, key)
        query_high, query_low = split(
            query_both[:BUCKETS] * query_both[BUCKETS:] * (even * FACTOR2)
        )
        key_high, key_low = split(key_both[:BUCKETS] * key_both[BUCKETS:] * FACTOR2)
        query_parts = jnp.concatenate([query_high, query_high, query_low], 0)
        key_parts = jnp.concatenate([key_high, key_low, key_high], 0)
        sketched = lax.dot_general(
            query_parts, key_parts, (((0,), (0,)), ((), ())), preferred_element_type=F32
        )
        weights = quartic(dot_nt(query, key)) - sketched * sketched
        near_ref[:, cols] = own_ref[:, cols] + dot_nn(weights.astype(BF16), value_ref[:, cols])


def query_kernel(hash_ref, sign_ref, query_ref, phi_ref):
    heads = query_ref.shape[1] // HD
    row = lax.broadcasted_iota(jnp.int32, (HD, HD), 0)
    base_bucket = row % BUCKETS
    shift = row // BUCKETS
    weight = jnp.where(shift == 0, 1.0, 2.0)
    pieces = []
    for level in range(2):
        hash_row = hash_ref[level : level + 1, :]
        sign_row = sign_ref[level : level + 1, :]
        pieces.append(sketch_rows(base_bucket, hash_row, sign_row))
        pieces.append(
            sketch_rows(
                (base_bucket + shift) % BUCKETS, hash_row, sign_row, weight if level == 0 else 1.0
            )
        )
    sketch = jnp.concatenate(pieces, 0)
    for head in range(heads):
        both = dot_nt(query_ref[:, head_cols(head)], sketch)
        first = both[:, :HD] * both[:, 2 * HD : 3 * HD] * FACTOR4
        second = both[:, HD : 2 * HD] * both[:, 3 * HD :]
        opposite = second[:, :BUCKETS]
        opposite = jnp.concatenate(
            [opposite[:, BUCKETS // 2 :], opposite[:, : BUCKETS // 2]], 1
        )
        last = first[:, :BUCKETS] * opposite
        phi_ref[head, :, :HD] = (first * second).astype(BF16)
        phi_ref[head, :, HD:] = last.astype(BF16)


def far_kernel(phi_ref, mine_ref, theirs_ref, near_ref, gain_ref, out_ref):
    core, chip = place()
    per_piece = mine_ref.shape[1]
    for side, far_ref in ((core, mine_ref), (1 - core, theirs_ref)):
        for piece in range(PLANE):
            for inner in range(per_piece):
                head = head_of(side, chip ^ piece, inner, per_piece)
                cols = cols_of(head)
                mixed = near_ref[:, cols] + dot_nn(phi_ref[head], far_ref[piece, inner])
                mean_square = jnp.mean(mixed * mixed, axis=-1, keepdims=True)
                out_ref[:, cols] = (
                    mixed * lax.rsqrt(mean_square + EPS) * gain_ref[:, cols]
                ).astype(BF16)


def kernel_call(body, out_shape, *args):
    return pl.pallas_call(
        body,
        out_shape=out_shape,
        compiler_params=pltpu.CompilerParams(vmem_limit_bytes=16 * 1024 * 1024),
    )(*args)


def from_behind(block, axis, distance):
    devices = range(lax.axis_size(axis))
    route = [(i - distance, i) for i in devices if i - distance in devices]
    return lax.ppermute(block, axis, route)


def swap(block, mask):
    route = [(i, i ^ mask) for i in range(lax.axis_size("seq"))]
    return lax.ppermute(block, "seq", route)


def earlier_chips(keep, send):
    devices = lax.axis_size("seq")
    index = lax.axis_index("seq")
    chip = (index // CORES) % PLANE
    summed = keep + swap(send, 1)
    shares = [summed[0]] + [
        swap(summed[m].astype(BF16), CORES * m).astype(F32) for m in range(1, PLANE)
    ]
    total = shares[0] + shares[1] + shares[2] + shares[3]
    earlier = jnp.zeros_like(total)
    mask = CORES * PLANE
    while mask < devices:
        got = swap(total.astype(BF16), mask).astype(F32)
        earlier = earlier + jnp.where((index & mask) != 0, got, 0.0)
        total = total + got
        mask *= 2
    prefixes = []
    for m in range(PLANE):
        prefix = earlier
        for other in range(PLANE):
            if other != m:
                prefix = prefix + jnp.where((chip ^ other) < (chip ^ m), shares[other], 0.0)
        prefixes.append(prefix.astype(BF16))
    mine = jnp.stack([prefixes[0]] + [swap(prefixes[m], CORES * m) for m in range(1, PLANE)], 0)
    return mine, swap(mine, 1)


def block_program(queries, keys, values, out_gain, hash_ids, sign_ids):
    rows, width = queries.shape
    heads = width // HD
    near_shape = jax.ShapeDtypeStruct((rows, width), F32)
    half_shape = jax.ShapeDtypeStruct((PLANE, heads // (CORES * PLANE), FEATURES, HD), F32)

    key_prev = from_behind(keys, "seq", 1)
    value_prev = from_behind(values, "seq", 1)
    keep, send = kernel_call(state_kernel, (half_shape, half_shape), hash_ids, sign_ids, keys, values)
    mine, theirs = earlier_chips(keep, send)
    near = kernel_call(own_kernel, near_shape, queries, keys, values)
    phi = kernel_call(
        query_kernel,
        jax.ShapeDtypeStruct((heads, rows, FEATURES), BF16),
        hash_ids,
        sign_ids,
        queries,
    )
    near = kernel_call(
        before_kernel, near_shape, hash_ids, sign_ids, queries, key_prev, value_prev, near
    )
    return kernel_call(
        far_kernel,
        jax.ShapeDtypeStruct((rows, width), BF16),
        phi,
        mine,
        theirs,
        near,
        out_gain.reshape(1, width),
    )


def solution(mesh):
    in_specs = (
        P(("grp", "seq"), "head"),
        P(("grp", "seq"), "head"),
        P(("grp", "seq"), "head"),
        P("head"),
        P(),
        P(),
    )
    out_specs = P(("grp", "seq"), "head")
    return jax.shard_map(
        block_program, mesh=mesh, in_specs=in_specs, out_specs=out_specs, check_vma=False
    )
```

time: 82.7 us -> 69.1 us (0.84)
  the two profiles are of different devices: /device:TPU:16 before, /device:TPU:25 now
where the time goes in v2:
time: 69.1 us; the launch traced here: 68.8 us
  starting transfers between devices  34.4 us (50%)
  Pallas kernels  16.7 us (24%)
  waiting for transfers between devices  14.1 us (20%)
  other arithmetic  1.97 us (3%)
  local copies, waits for them, and re-layouts  1.41 us (2%)
    ppermute x10, starting transfers between devices, swap(): return lax.ppermute(block, 'seq', route)  28.1 us
    pallas_call x5, Pallas kernels, kernel_call(): pl.pallas_call(body, out_shape=out_shape, compiler_params=pltpu.CompilerP...  16.7 us
    ppermute x10, waiting for transfers between devices, swap(): return lax.ppermute(block, 'seq', route)  14.1 us
    ppermute x2, starting transfers between devices, from_behind(): return lax.ppermute(block, axis, route)  6.32 us
    unnamed x14, local copies, waits for them, and re-layouts  1.39 us
  transfers between devices with their start and end apart: 12, of which 7 were waited for; matrix products, arithmetic and copies ran while one was open for 3% of the time, Pallas kernels for 15%

profile of v2, /device:TPU:25, one launch (start us, length us, event | category | flops | bytes accessed | tf_op | source)
XLA Modules:
  0.0 68.8 jit_solution(9736443865217220220)
XLA Ops:
  0.0 0.0 copy-start.1
  0.0 0.7 copy-done.1
  0.7 0.0 copy-start.3
  0.7 0.7 copy-done.3
  1.4 4.8 %shard_map.65 = (f32[4,2,144,128]{3,2,1,0:T(8,128)S(1)}, f32[4,2,144,128]{3,2,1,0:T(8,128)S(1)}) custom-call(s32[2,128]{1,0:T(2,128)S(1)} %copy-done.1, s32[2,128]{1,0:T(2,128)S(1)} %copy-done.3, bf16[256,2048]{1,0:T(8,128)(2,1)} %key_ref.3, bf16[256,2048]{1,0:T(8,128)(2,1)} %value_ref.3), custom_call_target="tpu_custom_call" | custom-call | tf_op jit(solution)/shard_map/pallas_call | solution.py:185
  6.1 0.7 %collective-permute-start = (f32[4,2,144,128]{3,2,1,0:T(8,128)S(1)}, f32[4,2,144,128]{3,2,1,0:T(8,128)S(1)}, u32[]{:S(2)}, u32[]{:S(2)}) collective-permute-start(f32[4,2,144,128]{3,2,1,0:T(8,128)S(1)} %get-tuple-element.8), channel_id=1, source_target_pairs={{0,1},{1,0},{2,3},{3,2},{4,5},{5,4},{6,7},{7,6},{8,9},{9,8},{10,11... | collective-permute-start | bytes 1769480 | tf_op jit(solution)/shard_map/ppermute | solution.py:200
  6.9 1.6 %collective-permute-done = f32[4,2,144,128]{3,2,1,0:T(8,128)S(1)} collective-permute-done((f32[4,2,144,128]{3,2,1,0:T(8,128)S(1)}, f32[4,2,144,128]{3,2,1,0:T(8,128)S(1)}, u32[]{:S(2)}, u32[]{:S(2)}) %collective-permute-start) | collective-permute-done | bytes 589856 | tf_op jit(solution)/shard_map/ppermute | solution.py:200
  8.5 0.1 fusion.17
  8.6 0.0 copy-start.6
  8.6 0.0 copy-start
  8.6 1.3 %collective-permute-start.1 = (bf16[2,144,128]{2,1,0:T(8,128)(2,1)S(1)}, bf16[2,144,128]{2,1,0:T(8,128)(2,1)S(1)}, u32[]{:S(2)}, u32[]{:S(2)}) collective-permute-start(bf16[2,144,128]{2,1,0:T(8,128)(2,1)S(1)} %get-tuple-element.16), channel_id=1, source_target_pairs={{0,2},{1,3},{2,0},{3,1},{4,6},{5,7},{6,4},{7,5},{8,10},{9,11},{10,... | collective-permute-start | bytes 221192 | tf_op jit(solution)/shard_map/ppermute | solution.py:200
  9.9 1.2 %collective-permute-start.2 = (bf16[2,144,128]{2,1,0:T(8,128)(2,1)S(1)}, bf16[2,144,128]{2,1,0:T(8,128)(2,1)S(1)}, u32[]{:S(2)}, u32[]{:S(2)}) collective-permute-start(bf16[2,144,128]{2,1,0:T(8,128)(2,1)S(1)} %get-tuple-element.15), channel_id=1, source_target_pairs={{0,4},{1,5},{2,6},{3,7},{4,0},{5,1},{6,2},{7,3},{8,12},{9,13},{10,... | collective-permute-start | bytes 221192 | tf_op jit(solution)/shard_map/ppermute | solution.py:200
  11.2 0.2 collective-permute-start.3
  11.4 0.6 collective-permute-done.1
  11.9 1.2 %collective-permute-done.2 = bf16[2,144,128]{2,1,0:T(8,128)(2,1)S(1)} collective-permute-done((bf16[2,144,128]{2,1,0:T(8,128)(2,1)S(1)}, bf16[2,144,128]{2,1,0:T(8,128)(2,1)S(1)}, u32[]{:S(2)}, u32[]{:S(2)}) %collective-permute-start.2) | collective-permute-done | bytes 73760 | tf_op jit(solution)/shard_map/ppermute | solution.py:200
  13.1 2.1 %collective-permute-done.3 = bf16[2,144,128]{2,1,0:T(8,128)(2,1)S(1)} collective-permute-done((bf16[2,144,128]{2,1,0:T(8,128)(2,1)S(1)}, bf16[2,144,128]{2,1,0:T(8,128)(2,1)S(1)}, u32[]{:S(2)}, u32[]{:S(2)}) %collective-permute-start.3) | collective-permute-done | bytes 73760 | tf_op jit(solution)/shard_map/ppermute | solution.py:200
  15.3 0.2 collective-permute-start.4
  15.5 4.4 %collective-permute-start.10 = (bf16[256,2048]{1,0:T(8,128)(2,1)}, bf16[256,2048]{1,0:T(8,128)(2,1)S(1)}, u32[]{:S(2)}, u32[]{:S(2)}) collective-permute-start(bf16[256,2048]{1,0:T(8,128)(2,1)} %key_ref.3), channel_id=1, source_target_pairs={{0,1},{1,2},{2,3},{3,4},{4,5},{5,6},{6,7},{7,8},{8,9},{9,10},{10,1... | collective-permute-start | bytes 3145736 | tf_op jit(solution)/shard_map/ppermute | solution.py:195
  20.0 1.9 %collective-permute-start.11 = (bf16[256,2048]{1,0:T(8,128)(2,1)}, bf16[256,2048]{1,0:T(8,128)(2,1)S(1)}, u32[]{:S(2)}, u32[]{:S(2)}) collective-permute-start(bf16[256,2048]{1,0:T(8,128)(2,1)} %value_ref.3), channel_id=1, source_target_pairs={{0,1},{1,2},{2,3},{3,4},{4,5},{5,6},{6,7},{7,8},{8,9},{9,10},{10,1... | collective-permute-start | bytes 3145736 | tf_op jit(solution)/shard_map/ppermute | solution.py:195
  21.9 0.0 collective-permute-done.4
  21.9 0.0 copy-done.6
  21.9 0.7 fusion.1
  22.6 0.1 collective-permute-start.5
  22.6 4.6 %collective-permute-done.5 = bf16[2,144,128]{2,1,0:T(8,128)(2,1)S(1)} collective-permute-done((bf16[2,144,128]{2,1,0:T(8,128)(2,1)}, bf16[2,144,128]{2,1,0:T(8,128)(2,1)S(1)}, u32[]{:S(2)}, u32[]{:S(2)}) %collective-permute-start.5) | collective-permute-done | bytes 73760 | tf_op jit(solution)/shard_map/ppermute | solution.py:200
  27.2 1.1 %fusion.14 = (bf16[2,144,128]{2,1,0:T(8,128)(2,1)S(1)}, bf16[2,144,128]{2,1,0:T(8,128)(2,1)S(1)}, bf16[2,144,128]{2,1,0:T(8,128)(2,1)S(1)}) fusion(bf16[2,144,128]{2,1,0:T(8,128)(2,1)S(1)} %collective-permute-done.2, bf16[2,144,128]{2,1,0:T(8,128)(2,1)S(1)} %collective-permute-done.3, f32[4,2,144,128]{3,2,1,0:T(8,128)} %copy-done.6, pred[]{:T(512)S(6)} %lt.48, ...), kind=kLoop, calls=%fused_computation.29 | loop fusion | flops 1069056 | bytes 737291 | tf_op jit(solution)/shard_map/convert_element_type | solution.py:225
  28.2 1.1 %collective-permute-start.6 = (bf16[2,144,128]{2,1,0:T(8,128)(2,1)S(1)}, bf16[2,144,128]{2,1,0:T(8,128)(2,1)S(1)}, u32[]{:S(2)}, u32[]{:S(2)}) collective-permute-start(bf16[2,144,128]{2,1,0:T(8,128)(2,1)S(1)} %get-tuple-element.11), channel_id=1, source_target_pairs={{0,2},{1,3},{2,0},{3,1},{4,6},{5,7},{6,4},{7,5},{8,10},{9,11},{10,... | collective-permute-start | bytes 221192 | tf_op jit(solution)/shard_map/ppermute | solution.py:200
  29.4 23.2 %collective-permute-start.7 = (bf16[2,144,128]{2,1,0:T(8,128)(2,1)S(1)}, bf16[2,144,128]{2,1,0:T(8,128)(2,1)S(1)}, u32[]{:S(2)}, u32[]{:S(2)}) collective-permute-start(bf16[2,144,128]{2,1,0:T(8,128)(2,1)S(1)} %get-tuple-element.12), channel_id=1, source_target_pairs={{0,4},{1,5},{2,6},{3,7},{4,0},{5,1},{6,2},{7,3},{8,12},{9,13},{10,... | collective-permute-start | bytes 221192 | tf_op jit(solution)/shard_map/ppermute | solution.py:200
  52.5 0.0 collective-permute-start.8
  52.5 0.1 fusion.15
  52.6 0.0 collective-permute-done.6
  52.6 1.6 %collective-permute-done.7 = bf16[2,144,128]{2,1,0:T(8,128)(2,1)S(1)} collective-permute-done((bf16[2,144,128]{2,1,0:T(8,128)(2,1)S(1)}, bf16[2,144,128]{2,1,0:T(8,128)(2,1)S(1)}, u32[]{:S(2)}, u32[]{:S(2)}) %collective-permute-start.7) | collective-permute-done | bytes 73760 | tf_op jit(solution)/shard_map/ppermute | solution.py:200
  54.3 2.4 %collective-permute-done.8 = bf16[2,144,128]{2,1,0:T(8,128)(2,1)S(1)} collective-permute-done((bf16[2,144,128]{2,1,0:T(8,128)(2,1)S(1)}, bf16[2,144,128]{2,1,0:T(8,128)(2,1)S(1)}, u32[]{:S(2)}, u32[]{:S(2)}) %collective-permute-start.8) | collective-permute-done | bytes 73760 | tf_op jit(solution)/shard_map/ppermute | solution.py:200
  56.7 0.0 copy-start.2
  56.7 0.0 copy-start.4
  56.7 0.1 collective-permute-start.9
  56.8 0.0 copy-done
  56.8 5.1 %shard_map.66.own_ref = f32[256,2048]{1,0:T(8,128)S(1)} custom-call(bf16[256,2048]{1,0:T(8,128)(2,1)S(1)} %copy-done, bf16[256,2048]{1,0:T(8,128)(2,1)} %key_ref.3, bf16[256,2048]{1,0:T(8,128)(2,1)} %value_ref.3), custom_call_target="tpu_custom_call" | custom-call | tf_op jit(solution)/shard_map/pallas_call | solution.py:185
  61.9 0.0 copy-done.2
  61.9 0.0 copy-done.4
  61.9 1.3 %shard_map.64.phi_ref = bf16[16,256,144]{2,1,0:T(8,128)(2,1)S(1)} custom-call(s32[2,128]{1,0:T(2,128)S(1)} %copy-done.2, s32[2,128]{1,0:T(2,128)S(1)} %copy-done.4, bf16[256,2048]{1,0:T(8,128)(2,1)S(1)} %copy-done), custom_call_target="tpu_custom_call" | custom-call | tf_op jit(solution)/shard_map/pallas_call | solution.py:185
  63.2 0.0 copy-start.5
  63.3 0.0 collective-permute-done.10.key_ref
  63.3 0.0 collective-permute-done.11.value_ref
  63.3 3.6 %shard_map.67.near_ref = f32[256,2048]{1,0:T(8,128)S(1)} custom-call(s32[2,128]{1,0:T(2,128)S(1)} %copy-done.2, s32[2,128]{1,0:T(2,128)S(1)} %copy-done.4, bf16[256,2048]{1,0:T(8,128)(2,1)S(1)} %copy-done, bf16[256,2048]{1,0:T(8,128)(2,1)S(1)} %collective-permute-done.10.key_ref, bf16[256,2048]{1,0:T(8,128)(2,1)S(1)} %collective-permute-done.11.value_ref, ...), custom_call_target="tpu_custom_call" | custom-call | tf_op jit(solution)/shard_map/pallas_call | solution.py:185
  66.9 0.0 collective-permute-done.9.theirs_ref
  66.9 0.0 copy-done.5
  66.9 1.9 %shard_map.68 = bf16[256,2048]{1,0:T(8,128)(2,1)} custom-call(bf16[16,256,144]{2,1,0:T(8,128)(2,1)S(1)} %shard_map.64.phi_ref, bf16[4,2,144,128]{3,2,1,0:T(8,128)(2,1)S(1)} %pad_maximum_fusion.mine_ref, bf16[4,2,144,128]{3,2,1,0:T(8,128)(2,1)S(1)} %collective-permute-done.9.theirs_ref, f32[256,2048]{1,0:T(8,128)S(1)} %shard_map.67.near_ref, ...), custom_call_target="tpu_custom_call" | custom-call | tf_op jit(solution)/shard_map/pallas_call | solution.py:185
  (3 shorter events, 0.1 us)
Async XLA Ops:
  0.0 0.7 copy-start.1
  0.7 0.7 copy-start.3
  6.1 2.4 %collective-permute-start = (f32[4,2,144,128]{3,2,1,0:T(8,128)S(1)}, f32[4,2,144,128]{3,2,1,0:T(8,128)S(1)}, u32[]{:S(2)}, u32[]{:S(2)}) collective-permute-start(f32[4,2,144,128]{3,2,1,0:T(8,128)S(1)} %get-tuple-element.8), channel_id=1, source_target_pairs={{0,1},{1,0},{2,3},{3,2},{4,5},{5,4},{6,7},{7,6},{8,9},{9,8},{10,11... | collective-permute-start | bytes 1769480 | tf_op jit(solution)/shard_map/ppermute | solution.py:200
  8.6 13.3 %copy-start.6 = (f32[4,2,144,128]{3,2,1,0:T(8,128)}, f32[4,2,144,128]{3,2,1,0:T(8,128)S(1)}, u32[]{:S(2)}) copy-start(f32[4,2,144,128]{3,2,1,0:T(8,128)S(1)} %get-tuple-element.10) | copy-start | bytes 1769476
  8.6 48.2 %copy-start = (bf16[256,2048]{1,0:T(8,128)(2,1)S(1)}, bf16[256,2048]{1,0:T(8,128)(2,1)}, u32[]{:S(2)}) copy-start(bf16[256,2048]{1,0:T(8,128)(2,1)} %query_ref.5) | copy-start | bytes 3145732
  8.6 3.3 %collective-permute-start.1 = (bf16[2,144,128]{2,1,0:T(8,128)(2,1)S(1)}, bf16[2,144,128]{2,1,0:T(8,128)(2,1)S(1)}, u32[]{:S(2)}, u32[]{:S(2)}) collective-permute-start(bf16[2,144,128]{2,1,0:T(8,128)(2,1)S(1)} %get-tuple-element.16), channel_id=1, source_target_pairs={{0,2},{1,3},{2,0},{3,1},{4,6},{5,7},{6,4},{7,5},{8,10},{9,11},{10,... | collective-permute-start | bytes 221192 | tf_op jit(solution)/shard_map/ppermute | solution.py:200
  9.9 3.2 %collective-permute-start.2 = (bf16[2,144,128]{2,1,0:T(8,128)(2,1)S(1)}, bf16[2,144,128]{2,1,0:T(8,128)(2,1)S(1)}, u32[]{:S(2)}, u32[]{:S(2)}) collective-permute-start(bf16[2,144,128]{2,1,0:T(8,128)(2,1)S(1)} %get-tuple-element.15), channel_id=1, source_target_pairs={{0,4},{1,5},{2,6},{3,7},{4,0},{5,1},{6,2},{7,3},{8,12},{9,13},{10,... | collective-permute-start | bytes 221192 | tf_op jit(solution)/shard_map/ppermute | solution.py:200
  11.2 4.1 %collective-permute-start.3 = (bf16[2,144,128]{2,1,0:T(8,128)(2,1)S(1)}, bf16[2,144,128]{2,1,0:T(8,128)(2,1)S(1)}, u32[]{:S(2)}, u32[]{:S(2)}) collective-permute-start(bf16[2,144,128]{2,1,0:T(8,128)(2,1)S(1)} %get-tuple-element.14), channel_id=1, source_target_pairs={{0,6},{1,7},{2,4},{3,5},{4,2},{5,3},{6,0},{7,1},{8,14},{9,15},{10,... | collective-permute-start | bytes 221192 | tf_op jit(solution)/shard_map/ppermute | solution.py:200
  15.3 6.6 %collective-permute-start.4 = (bf16[2,144,128]{2,1,0:T(8,128)(2,1)S(1)}, bf16[2,144,128]{2,1,0:T(8,128)(2,1)S(1)}, u32[]{:S(2)}, u32[]{:S(2)}) collective-permute-start(bf16[2,144,128]{2,1,0:T(8,128)(2,1)S(1)} %fusion.16), channel_id=1, source_target_pairs={{0,8},{1,9},{2,10},{3,11},{4,12},{5,13},{6,14},{7,15},{8,0},{9,1},... | collective-permute-start | bytes 221192 | tf_op jit(solution)/shard_map/ppermute | solution.py:200
  15.5 47.7 %collective-permute-start.10 = (bf16[256,2048]{1,0:T(8,128)(2,1)}, bf16[256,2048]{1,0:T(8,128)(2,1)S(1)}, u32[]{:S(2)}, u32[]{:S(2)}) collective-permute-start(bf16[256,2048]{1,0:T(8,128)(2,1)} %key_ref.3), channel_id=1, source_target_pairs={{0,1},{1,2},{2,3},{3,4},{4,5},{5,6},{6,7},{7,8},{8,9},{9,10},{10,1... | collective-permute-start | bytes 3145736 | tf_op jit(solution)/shard_map/ppermute | solution.py:195
  20.0 43.3 %collective-permute-start.11 = (bf16[256,2048]{1,0:T(8,128)(2,1)}, bf16[256,2048]{1,0:T(8,128)(2,1)S(1)}, u32[]{:S(2)}, u32[]{:S(2)}) collective-permute-start(bf16[256,2048]{1,0:T(8,128)(2,1)} %value_ref.3), channel_id=1, source_target_pairs={{0,1},{1,2},{2,3},{3,4},{4,5},{5,6},{6,7},{7,8},{8,9},{9,10},{10,1... | collective-permute-start | bytes 3145736 | tf_op jit(solution)/shard_map/ppermute | solution.py:195
  22.6 4.6 %collective-permute-start.5 = (bf16[2,144,128]{2,1,0:T(8,128)(2,1)}, bf16[2,144,128]{2,1,0:T(8,128)(2,1)S(1)}, u32[]{:S(2)}, u32[]{:S(2)}) collective-permute-start(bf16[2,144,128]{2,1,0:T(8,128)(2,1)} %fusion.1), channel_id=1, source_target_pairs={{0,16},{1,17},{2,18},{3,19},{4,20},{5,21},{6,22},{7,23},{8,24},{9,... | collective-permute-start | bytes 221192 | tf_op jit(solution)/shard_map/ppermute | solution.py:200
  28.2 24.4 %collective-permute-start.6 = (bf16[2,144,128]{2,1,0:T(8,128)(2,1)S(1)}, bf16[2,144,128]{2,1,0:T(8,128)(2,1)S(1)}, u32[]{:S(2)}, u32[]{:S(2)}) collective-permute-start(bf16[2,144,128]{2,1,0:T(8,128)(2,1)S(1)} %get-tuple-element.11), channel_id=1, source_target_pairs={{0,2},{1,3},{2,0},{3,1},{4,6},{5,7},{6,4},{7,5},{8,10},{9,11},{10,... | collective-permute-start | bytes 221192 | tf_op jit(solution)/shard_map/ppermute | solution.py:200
  29.4 24.9 %collective-permute-start.7 = (bf16[2,144,128]{2,1,0:T(8,128)(2,1)S(1)}, bf16[2,144,128]{2,1,0:T(8,128)(2,1)S(1)}, u32[]{:S(2)}, u32[]{:S(2)}) collective-permute-start(bf16[2,144,128]{2,1,0:T(8,128)(2,1)S(1)} %get-tuple-element.12), channel_id=1, source_target_pairs={{0,4},{1,5},{2,6},{3,7},{4,0},{5,1},{6,2},{7,3},{8,12},{9,13},{10,... | collective-permute-start | bytes 221192 | tf_op jit(solution)/shard_map/ppermute | solution.py:200
  52.5 4.1 %collective-permute-start.8 = (bf16[2,144,128]{2,1,0:T(8,128)(2,1)S(1)}, bf16[2,144,128]{2,1,0:T(8,128)(2,1)S(1)}, u32[]{:S(2)}, u32[]{:S(2)}) collective-permute-start(bf16[2,144,128]{2,1,0:T(8,128)(2,1)S(1)} %get-tuple-element.13), channel_id=1, source_target_pairs={{0,6},{1,7},{2,4},{3,5},{4,2},{5,3},{6,0},{7,1},{8,14},{9,15},{10,... | collective-permute-start | bytes 221192 | tf_op jit(solution)/shard_map/ppermute | solution.py:200
  56.7 5.2 %copy-start.2 = (s32[2,128]{1,0:T(2,128)S(1)}, s32[2,128]{1,0:T(2,128)}, u32[]{:S(2)}) copy-start(s32[2,128]{1,0:T(2,128)} %hash_ref.5) | copy-start | bytes 3076
  56.7 5.2 %copy-start.4 = (s32[2,128]{1,0:T(2,128)S(1)}, s32[2,128]{1,0:T(2,128)}, u32[]{:S(2)}) copy-start(s32[2,128]{1,0:T(2,128)} %sign_ref.5) | copy-start | bytes 3076
  56.7 10.2 %collective-permute-start.9 = (bf16[4,2,144,128]{3,2,1,0:T(8,128)(2,1)S(1)}, bf16[4,2,144,128]{3,2,1,0:T(8,128)(2,1)S(1)}, u32[]{:S(2)}, u32[]{:S(2)}) collective-permute-start(bf16[4,2,144,128]{3,2,1,0:T(8,128)(2,1)S(1)} %pad_maximum_fusion.mine_ref), channel_id=1, source_target_pairs={{0,1},{1,0},{2,3},{3,2},{4,5},{5,4},{6,7},{7,6},{8,9},{9,8},{10,11... | collective-permute-start | bytes 884744 | tf_op jit(solution)/shard_map/ppermute | solution.py:200
  63.2 3.7 %copy-start.5 = (f32[2048]{0:T(1024)S(1)}, f32[2048]{0:T(1024)}, u32[]{:S(2)}) copy-start(f32[2048]{0:T(1024)} %param.9) | copy-start | bytes 24580

commit v3 on v1

v3 whole, which is shorter than its diff:
```python
import functools

import jax
import jax.numpy as jnp
from jax import lax
from jax.experimental import pallas as pl
from jax.experimental.pallas import tpu as pltpu
from jax.sharding import PartitionSpec as P


HD = 128
BUCKETS = 16
SHIFTS = BUCKETS // 2 + 1
FEATURES = SHIFTS * BUCKETS
FACTOR4 = (0.75 * (BUCKETS / HD) ** 0.5) ** 4
FACTOR2 = (0.75 * (BUCKETS / HD) ** 0.5) ** 2
EPS = 1e-06
CORES = 2
PLANE = 4
CHUNKS = 4
BF16 = jnp.bfloat16
F32 = jnp.float32
VMEM_LIMIT = 12 * 1024 * 1024
IN_HBM = pl.BlockSpec(memory_space=pltpu.HBM)


def dot_nt(a, b):
    return lax.dot_general(a, b, (((1,), (1,)), ((), ())), preferred_element_type=F32)


def dot_nn(a, b):
    return lax.dot_general(a, b, (((1,), (0,)), ((), ())), preferred_element_type=F32)


def dot_tn(a, b):
    return lax.dot_general(a, b, (((0,), (0,)), ((), ())), preferred_element_type=F32)


def sketch_rows(buckets, hash_row, sign_row, weight=1.0):
    signs = (2 * sign_row - 1).astype(F32) * weight
    return jnp.where(hash_row == buckets, signs, 0.0).astype(BF16)


def head_cols(head):
    return pl.ds(head * HD, HD)


def place():
    index = lax.axis_index("seq")
    return index % CORES, (index // CORES) % PLANE


def side_of(half):
    core, _ = place()
    return 1 - core if half == 0 else core


def dynamic_cols(start, width):
    return pl.ds(pl.multiple_of(start, HD), width)


def quartic(scores):
    squared = scores * scores * (1.0 / HD)
    return squared * squared


def state_kernel(
    hash_hbm,
    sign_hbm,
    query_hbm,
    key_hbm,
    value_hbm,
    send_ref,
    keep_ref,
    hash_ref,
    sign_ref,
    query_0_ref,
    query_1_ref,
    key_0_ref,
    key_1_ref,
    value_0_ref,
    value_1_ref,
    sems,
):
    _, chip = place()
    per_piece = keep_ref.shape[1]
    half_width = key_0_ref.shape[1]
    half_heads = half_width // HD
    chunk_heads = max(half_heads // CHUNKS, 1)
    chunk = chunk_heads * HD
    chunks = half_heads // chunk_heads
    copies = [
        pltpu.make_async_copy(hash_hbm, hash_ref, sems.at[0]),
        pltpu.make_async_copy(sign_hbm, sign_ref, sems.at[1]),
    ]
    halves = ((key_0_ref, value_0_ref), (key_1_ref, value_1_ref))
    for half, refs in enumerate(halves):
        for part in range(chunks):
            cols = dynamic_cols(side_of(half) * half_width + part * chunk, chunk)
            inner = pl.ds(part * chunk, chunk)
            for hbm, ref in zip((key_hbm, value_hbm), refs):
                copies.append(
                    pltpu.make_async_copy(hbm.at[:, cols], ref.at[:, inner], sems.at[len(copies)])
                )
    for half, ref in enumerate((query_0_ref, query_1_ref)):
        cols = dynamic_cols(side_of(half) * half_width, half_width)
        copies.append(pltpu.make_async_copy(query_hbm.at[:, cols], ref, sems.at[len(copies)]))
    for copy in copies:
        copy.start()
    copies[0].wait()
    copies[1].wait()
    row = lax.broadcasted_iota(jnp.int32, (FEATURES, HD), 0)
    buckets = (row + row // BUCKETS) % BUCKETS
    sketch = jnp.concatenate(
        [
            sketch_rows(buckets, hash_ref[level : level + 1, :], sign_ref[level : level + 1, :])
            for level in range(2)
        ],
        0,
    )
    for half, (key_ref, value_ref) in enumerate(halves):
        total_ref = (send_ref, keep_ref)[half]
        for head in range(half_heads):
            if head % chunk_heads == 0:
                first = 2 + 2 * (half * chunks + head // chunk_heads)
                copies[first].wait()
                copies[first + 1].wait()
            cols = head_cols(head)
            both = dot_nt(sketch, key_ref[:, cols])
            level = both[:FEATURES] * both[FEATURES:]
            base = level[:BUCKETS] * FACTOR4
            phi = jnp.concatenate(
                [base * level[d * BUCKETS : (d + 1) * BUCKETS] for d in range(SHIFTS)], 0
            ).astype(BF16)
            total_ref[(head // per_piece) ^ chip, head % per_piece] = dot_nn(
                phi, value_ref[:, cols]
            )
    copies[-2].wait()
    copies[-1].wait()


def query_kernel(hash_ref, sign_ref, query_0_ref, query_1_ref, phi_ref):
    half_heads = query_0_ref.shape[1] // HD
    row = lax.broadcasted_iota(jnp.int32, (HD, HD), 0)
    base_bucket = row % BUCKETS
    shift = row // BUCKETS
    weight = jnp.where(shift == 0, 1.0, 2.0)
    pieces = []
    for level in range(2):
        hash_row = hash_ref[level : level + 1, :]
        sign_row = sign_ref[level : level + 1, :]
        pieces.append(sketch_rows(base_bucket, hash_row, sign_row))
        pieces.append(
            sketch_rows(
                (base_bucket + shift) % BUCKETS, hash_row, sign_row, weight if level == 0 else 1.0
            )
        )
    sketch = jnp.concatenate(pieces, 0)
    for half, query_ref in enumerate((query_0_ref, query_1_ref)):
        for head in range(half_heads):
            both = dot_nt(query_ref[:, head_cols(head)], sketch)
            first = both[:, :HD] * both[:, 2 * HD : 3 * HD] * FACTOR4
            second = both[:, HD : 2 * HD] * both[:, 3 * HD :]
            opposite = second[:, :BUCKETS]
            opposite = jnp.concatenate(
                [opposite[:, BUCKETS // 2 :], opposite[:, : BUCKETS // 2]], 1
            )
            last = first[:, :BUCKETS] * opposite
            phi_ref[half * half_heads + head, :, :HD] = (first * second).astype(BF16)
            phi_ref[half * half_heads + head, :, HD:] = last.astype(BF16)


def own_kernel(query_ref, key_ref, value_ref, near_ref):
    rows = query_ref.shape[0]
    half = rows // 2
    allowed = lax.broadcasted_iota(jnp.int32, (rows, half), 1) <= lax.broadcasted_iota(
        jnp.int32, (rows, half), 0
    )
    for head in range(query_ref.shape[1] // HD):
        cols = head_cols(head)
        query = query_ref[:, cols]
        left = jnp.where(allowed, quartic(dot_nt(query, key_ref[:half, cols])), 0.0)
        right = jnp.where(
            allowed[:half], quartic(dot_nt(query[half:], key_ref[half:, cols])), 0.0
        )
        near = dot_nn(left.astype(BF16), value_ref[:half, cols])
        near_ref[:half, cols] = near[:half]
        near_ref[half:, cols] = near[half:] + dot_nn(right.astype(BF16), value_ref[half:, cols])


def split(x):
    high = x.astype(BF16)
    low = (x - high.astype(F32)).astype(BF16)
    return high, low


def weights_kernel(half, hash_ref, sign_ref, query_ref, key_ref, weight_ref):
    core, _ = place()
    even = jnp.where(core == 0, 1.0, 0.0)
    half_width = query_ref.shape[1]
    row = lax.broadcasted_iota(jnp.int32, (BUCKETS, HD), 0)
    sketch = jnp.concatenate(
        [
            sketch_rows(row, hash_ref[level : level + 1, :], sign_ref[level : level + 1, :])
            for level in range(2)
        ],
        0,
    )
    for head in range(half_width // HD):
        query = query_ref[:, head_cols(head)]
        key = key_ref[:, dynamic_cols(side_of(half) * half_width + head * HD, HD)]
        query_both = dot_nt(sketch, query)
        key_both = dot_nt(sketch, key)
        query_high, query_low = split(
            query_both[:BUCKETS] * query_both[BUCKETS:] * (even * FACTOR2)
        )
        key_high, key_low = split(key_both[:BUCKETS] * key_both[BUCKETS:] * FACTOR2)
        query_parts = jnp.concatenate([query_high, query_high, query_low], 0)
        key_parts = jnp.concatenate([key_high, key_low, key_high], 0)
        sketched = dot_tn(query_parts, key_parts)
        weights = quartic(dot_nt(query, key)) - sketched * sketched
        weight_ref[head] = weights.astype(BF16)


def values_kernel(weight_ref, value_ref, own_ref, near_ref):
    for head in range(weight_ref.shape[0]):
        cols = head_cols(head)
        near_ref[:, cols] = own_ref[:, cols] + dot_nn(weight_ref[head], value_ref[:, cols])


def far_kernel(
    phi_ref, theirs_ref, mine_ref, near_0_ref, near_1_ref, gain_ref, out_hbm, out_ref, sems
):
    _, chip = place()
    per_piece = mine_ref.shape[1]
    half_width = near_0_ref.shape[1]
    half_heads = half_width // HD
    width = per_piece * HD
    copies = []
    for half, (far_ref, near_ref) in enumerate(
        ((theirs_ref, near_0_ref), (mine_ref, near_1_ref))
    ):
        for piece in range(PLANE):
            slot = half * PLANE + piece
            start = side_of(half) * half_width + (chip ^ piece) * width
            for inner in range(per_piece):
                head = (chip ^ piece) * per_piece + inner
                mixed = near_ref[:, dynamic_cols(head * HD, HD)] + dot_nn(
                    phi_ref[half * half_heads + head], far_ref[piece, inner]
                )
                mean_square = jnp.mean(mixed * mixed, axis=-1, keepdims=True)
                gain = gain_ref[:, dynamic_cols(start + inner * HD, HD)]
                out_ref[slot, :, head_cols(inner)] = (
                    mixed * lax.rsqrt(mean_square + EPS) * gain
                ).astype(BF16)
            copies.append(
                pltpu.make_async_copy(
                    out_ref.at[slot], out_hbm.at[:, dynamic_cols(start, width)], sems.at[slot]
                )
            )
            copies[-1].start()
    for copy in copies:
        copy.wait()


def kernel_call(body, out_shape, *args, space=pltpu.VMEM, **options):
    return pl.pallas_call(
        body,
        out_shape=out_shape,
        compiler_params=pltpu.CompilerParams(vmem_limit_bytes=VMEM_LIMIT),
        **options,
    )(*[pltpu.with_memory_space_constraint(arg, space) for arg in args])


def from_behind(block, axis, distance):
    devices = range(lax.axis_size(axis))
    route = [(i - distance, i) for i in devices if i - distance in devices]
    return lax.ppermute(block, axis, route)


def swap(block, mask):
    route = [(i, i ^ mask) for i in range(lax.axis_size("seq"))]
    return lax.ppermute(block, "seq", route)


def chip_sum_kernel(keep_ref, got_ref, own_ref, *share_refs):
    own_ref[...] = keep_ref[0] + got_ref[0]
    for piece, share_ref in enumerate(share_refs, 1):
        share_ref[...] = (keep_ref[piece] + got_ref[piece]).astype(BF16)


def plane_sum_kernel(own_ref, *refs):
    share_refs, (total_ref, sent_ref) = refs[:-2], refs[-2:]
    total = own_ref[...]
    for share_ref in share_refs:
        total = total + share_ref[...].astype(F32)
    total_ref[...] = total
    sent_ref[...] = total.astype(BF16)


def later_half(mask):
    return (lax.axis_index("seq") // mask) % 2


def first_across_kernel(mask, total_ref, got_ref, earlier_ref, more_ref, sent_ref):
    got = got_ref[...].astype(F32)
    earlier_ref[...] = jnp.where(later_half(mask) == 1, got, 0.0)
    total = total_ref[...] + got
    more_ref[...] = total
    sent_ref[...] = total.astype(BF16)


def next_across_kernel(mask, earlier_before_ref, total_ref, got_ref, earlier_ref, more_ref, sent_ref):
    got = got_ref[...].astype(F32)
    earlier_ref[...] = earlier_before_ref[...] + jnp.where(later_half(mask) == 1, got, 0.0)
    total = total_ref[...] + got
    more_ref[...] = total
    sent_ref[...] = total.astype(BF16)


def prefix_kernel(mask, earlier_ref, got_ref, *refs):
    _, chip = place()
    share_refs, prefix_refs = refs[:PLANE], refs[PLANE:]
    earlier = earlier_ref[...] + jnp.where(later_half(mask) == 1, got_ref[...].astype(F32), 0.0)
    shares = [share_ref[...].astype(F32) for share_ref in share_refs]
    for piece, prefix_ref in enumerate(prefix_refs):
        prefix = earlier
        for other in range(PLANE):
            if other != piece:
                ahead = (chip ^ other) < (chip ^ piece)
                prefix = prefix + jnp.where(ahead, shares[other], 0.0)
        prefix_ref[...] = prefix.astype(BF16)


def stack_kernel(*refs):
    piece_refs, all_ref = refs[:-1], refs[-1]
    for piece, piece_ref in enumerate(piece_refs):
        all_ref[piece] = piece_ref[...]


def earlier_chips(keep, send):
    devices = lax.axis_size("seq")
    dims = keep.shape[1:]
    wide, narrow = pltpu.VMEM(dims, F32), pltpu.VMEM(dims, BF16)
    own, *sent = kernel_call(
        chip_sum_kernel, (wide,) + (narrow,) * (PLANE - 1), keep, swap(send, 1)
    )
    shares = [own] + [swap(block, CORES * m) for m, block in enumerate(sent, 1)]
    total, block = kernel_call(plane_sum_kernel, (wide, narrow), *shares)
    mask = CORES * PLANE
    got = swap(block, mask)
    earlier, total, block = kernel_call(
        functools.partial(first_across_kernel, mask), (wide, wide, narrow), total, got
    )
    mask *= 2
    got = swap(block, mask)
    while mask * 2 < devices:
        earlier, total, block = kernel_call(
            functools.partial(next_across_kernel, mask), (wide, wide, narrow), earlier, total, got
        )
        mask *= 2
        got = swap(block, mask)
    prefixes = kernel_call(
        functools.partial(prefix_kernel, mask), (narrow,) * PLANE, earlier, got, *shares
    )
    mine = kernel_call(
        stack_kernel,
        pltpu.VMEM((PLANE,) + dims, BF16),
        prefixes[0],
        *[swap(prefixes[m], CORES * m) for m in range(1, PLANE)],
    )
    return mine, swap(mine, 1)


def block_program(queries, keys, values, out_gain, hash_ids, sign_ids):
    rows, width = queries.shape
    heads = width // HD
    half_heads = heads // 2
    half_state = pltpu.VMEM((PLANE, heads // (CORES * PLANE), FEATURES, HD), F32)
    half_rows = pltpu.VMEM((rows, width // 2), BF16)
    half_near = pltpu.VMEM((rows, width // 2), F32)
    id_shape = pltpu.VMEM(hash_ids.shape, hash_ids.dtype)

    key_prev = from_behind(keys, "seq", 1)
    send, keep, hash_near, sign_near, query_0, query_1, key_0, key_1, value_0, value_1 = kernel_call(
        state_kernel,
        (half_state, half_state, id_shape, id_shape) + (half_rows,) * 6,
        hash_ids,
        sign_ids,
        queries,
        keys,
        values,
        space=pltpu.HBM,
        in_specs=[IN_HBM] * 5,
        scratch_shapes=[pltpu.SemaphoreType.DMA((4 + 4 * CHUNKS,))],
    )
    value_prev_1 = from_behind(value_0, "seq", 1)
    value_prev_0 = from_behind(value_1, "seq", 1)
    mine, theirs = earlier_chips(keep, send)
    phi = kernel_call(
        query_kernel,
        pltpu.VMEM((heads, rows, FEATURES), BF16),
        hash_near,
        sign_near,
        query_0,
        query_1,
    )
    near = []
    for half, query, key, value, value_prev in (
        (0, query_0, key_0, value_0, value_prev_0),
        (1, query_1, key_1, value_1, value_prev_1),
    ):
        own = kernel_call(own_kernel, half_near, query, key, value)
        weights = kernel_call(
            functools.partial(weights_kernel, half),
            pltpu.VMEM((half_heads, rows, rows), BF16),
            hash_near,
            sign_near,
            query,
            key_prev,
        )
        near.append(kernel_call(values_kernel, half_near, weights, value_prev, own))
    return kernel_call(
        far_kernel,
        pltpu.HBM((rows, width), BF16),
        phi,
        theirs,
        mine,
        *near,
        out_gain.reshape(1, width),
        out_specs=IN_HBM,
        scratch_shapes=[
            pltpu.VMEM((CORES * PLANE, rows, width // (CORES * PLANE)), BF16),
            pltpu.SemaphoreType.DMA((CORES * PLANE,)),
        ],
    )


def solution(mesh):
    in_specs = (
        P(("grp", "seq"), "head"),
        P(("grp", "seq"), "head"),
        P(("grp", "seq"), "head"),
        P("head"),
        P(),
        P(),
    )
    out_specs = P(("grp", "seq"), "head")
    return jax.shard_map(
        block_program, mesh=mesh, in_specs=in_specs, out_specs=out_specs, check_vma=False
    )
```

time: 82.7 us -> 66.2 us (0.80)
  the two profiles are of different devices: /device:TPU:16 before, /device:TPU:29 now
where the time goes in v3:
time: 66.2 us; the launch traced here: 66 us
  waiting for transfers between devices  24.4 us (37%)
  starting transfers between devices  24.2 us (37%)
  Pallas kernels  17.1 us (26%)
    ppermute x10, waiting for transfers between devices, swap(): return lax.ppermute(block, 'seq', route)  24.3 us
    ppermute x10, starting transfers between devices, swap(): return lax.ppermute(block, 'seq', route)  17.4 us
    pallas_call x14, Pallas kernels, kernel_call(): pl.pallas_call(body, out_shape=out_shape, compiler_params=pltpu.CompilerP...  17.1 us
    ppermute x3, starting transfers between devices, from_behind(): return lax.ppermute(block, axis, route)  6.85 us
  transfers between devices with their start and end apart: 13, of which 7 were waited for; matrix products, arithmetic and copies ran while one was open for 0% of the time, Pallas kernels for 15%

profile of v3, /device:TPU:29, one launch (start us, length us, event | category | flops | bytes accessed | tf_op | source)
XLA Modules:
  0.0 66.0 jit_solution(4556622799217294642)
XLA Ops:
  0.0 0.0 copy-start.1
  0.0 5.7 %shard_map.64 = (f32[4,2,144,128]{3,2,1,0:T(8,128)S(1)}, f32[4,2,144,128]{3,2,1,0:T(8,128)S(1)}, s32[2,128]{1,0:T(2,128)S(1)}, s32[2,128]{1,0:T(2,128)S(1)}, bf1...) custom-call(s32[2,128]{1,0:T(2,128)} %hash_hbm.1, ...), custom_call_target="tpu_custom_call" | custom-call | tf_op jit(solution)/shard_map/pallas_call | solution.py:267
  5.7 0.7 %collective-permute-start = (f32[4,2,144,128]{3,2,1,0:T(8,128)S(1)}, f32[4,2,144,128]{3,2,1,0:T(8,128)S(1)}, u32[]{:S(2)}, u32[]{:S(2)}) collective-permute-start(f32[4,2,144,128]{3,2,1,0:T(8,128)S(1)} %get-tuple-element.32), channel_id=1, source_target_pairs={{0,1},{1,0},{2,3},{3,2},{4,5},{5,4},{6,7},{7,6},{8,9},{9,8},{10,11... | collective-permute-start | bytes 1769480 | tf_op jit(solution)/shard_map/ppermute | solution.py:283
  6.4 0.0 copy-done.1
  6.4 3.0 %collective-permute-start.10 = (bf16[256,2048]{1,0:T(8,128)(2,1)S(1)}, bf16[256,2048]{1,0:T(8,128)(2,1)S(1)}, u32[]{:S(2)}, u32[]{:S(2)}) collective-permute-start(bf16[256,2048]{1,0:T(8,128)(2,1)S(1)} %copy-done.1), channel_id=1, source_target_pairs={{0,1},{1,2},{2,3},{3,4},{4,5},{5,6},{6,7},{7,8},{8,9},{9,10},{10,1... | collective-permute-start | bytes 3145736 | tf_op jit(solution)/shard_map/ppermute | solution.py:278
  9.5 0.0 collective-permute-done.got_ref
  9.5 0.1 shard_map.66
  9.6 0.1 collective-permute-start.1
  9.7 1.4 %collective-permute-start.2 = (bf16[2,144,128]{2,1,0:T(8,128)(2,1)S(1)}, bf16[2,144,128]{2,1,0:T(8,128)(2,1)S(1)}, u32[]{:S(2)}, u32[]{:S(2)}) collective-permute-start(bf16[2,144,128]{2,1,0:T(8,128)(2,1)S(1)} %get-tuple-element.35), channel_id=1, source_target_pairs={{0,4},{1,5},{2,6},{3,7},{4,0},{5,1},{6,2},{7,3},{8,12},{9,13},{10,... | collective-permute-start | bytes 221192 | tf_op jit(solution)/shard_map/ppermute | solution.py:283
  11.1 1.2 %collective-permute-start.3 = (bf16[2,144,128]{2,1,0:T(8,128)(2,1)S(1)}, bf16[2,144,128]{2,1,0:T(8,128)(2,1)S(1)}, u32[]{:S(2)}, u32[]{:S(2)}) collective-permute-start(bf16[2,144,128]{2,1,0:T(8,128)(2,1)S(1)} %get-tuple-element.36), channel_id=1, source_target_pairs={{0,6},{1,7},{2,4},{3,5},{4,2},{5,3},{6,0},{7,1},{8,14},{9,15},{10,... | collective-permute-start | bytes 221192 | tf_op jit(solution)/shard_map/ppermute | solution.py:283
  12.3 12.3 %collective-permute-done.1.refs_0_.refs_1_ = bf16[2,144,128]{2,1,0:T(8,128)(2,1)S(1)} collective-permute-done((bf16[2,144,128]{2,1,0:T(8,128)(2,1)S(1)}, bf16[2,144,128]{2,1,0:T(8,128)(2,1)S(1)}, u32[]{:S(2)}, u32[]{:S(2)}) %collective-permute-start.1) | collective-permute-done | bytes 73760 | tf_op jit(solution)/shard_map/ppermute | solution.py:283
  24.6 0.4 collective-permute-done.2.refs_1_.refs_2_
  25.0 1.1 %collective-permute-done.3.refs_2_.refs_3_ = bf16[2,144,128]{2,1,0:T(8,128)(2,1)S(1)} collective-permute-done((bf16[2,144,128]{2,1,0:T(8,128)(2,1)S(1)}, bf16[2,144,128]{2,1,0:T(8,128)(2,1)S(1)}, u32[]{:S(2)}, u32[]{:S(2)}) %collective-permute-start.3) | collective-permute-done | bytes 73760 | tf_op jit(solution)/shard_map/ppermute | solution.py:283
  26.1 1.0 %collective-permute-start.4 = (bf16[2,144,128]{2,1,0:T(8,128)(2,1)S(1)}, bf16[2,144,128]{2,1,0:T(8,128)(2,1)S(1)}, u32[]{:S(2)}, u32[]{:S(2)}) collective-permute-start(bf16[2,144,128]{2,1,0:T(8,128)(2,1)S(1)} %get-tuple-element.38), channel_id=1, source_target_pairs={{0,8},{1,9},{2,10},{3,11},{4,12},{5,13},{6,14},{7,15},{8,0},{9,1},... | collective-permute-start | bytes 221192 | tf_op jit(solution)/shard_map/ppermute | solution.py:283
  27.2 1.9 %collective-permute-start.12 = (bf16[256,1024]{1,0:T(8,128)(2,1)S(1)}, bf16[256,1024]{1,0:T(8,128)(2,1)S(1)}, u32[]{:S(2)}, u32[]{:S(2)}) collective-permute-start(bf16[256,1024]{1,0:T(8,128)(2,1)S(1)} %get-tuple-element.47.value_ref), channel_id=1, source_target_pairs={{0,1},{1,2},{2,3},{3,4},{4,5},{5,6},{6,7},{7,8},{8,9},{9,10},{10,1... | collective-permute-start | bytes 1572872 | tf_op jit(solution)/shard_map/ppermute | solution.py:278
  29.1 1.9 %collective-permute-start.11 = (bf16[256,1024]{1,0:T(8,128)(2,1)S(1)}, bf16[256,1024]{1,0:T(8,128)(2,1)S(1)}, u32[]{:S(2)}, u32[]{:S(2)}) collective-permute-start(bf16[256,1024]{1,0:T(8,128)(2,1)S(1)} %get-tuple-element.45.value_ref), channel_id=1, source_target_pairs={{0,1},{1,2},{2,3},{3,4},{4,5},{5,6},{6,7},{7,8},{8,9},{9,10},{10,1... | collective-permute-start | bytes 1572872 | tf_op jit(solution)/shard_map/ppermute | solution.py:278
  31.0 0.0 collective-permute-done.4.got_ref
  31.0 0.7 %shard_map.68 = (f32[2,144,128]{2,1,0:T(8,128)S(1)}, f32[2,144,128]{2,1,0:T(8,128)}, bf16[2,144,128]{2,1,0:T(8,128)(2,1)S(1)}) custom-call(f32[2,144,128]{2,1,0:T(8,128)S(1)} %get-tuple-element.37.total_ref, bf16[2,144,128]{2,1,0:T(8,128)(2,1)S(1)} %collective-permute-done.4.got_ref), custom_call_target="tpu_custom_call" | custom-call | tf_op jit(solution)/shard_map/pallas_call | solution.py:267
  31.7 0.0 collective-permute-start.5
  31.7 4.4 %collective-permute-done.5.got_ref = bf16[2,144,128]{2,1,0:T(8,128)(2,1)S(1)} collective-permute-done((bf16[2,144,128]{2,1,0:T(8,128)(2,1)S(1)}, bf16[2,144,128]{2,1,0:T(8,128)(2,1)S(1)}, u32[]{:S(2)}, u32[]{:S(2)}) %collective-permute-start.5) | collective-permute-done | bytes 73760 | tf_op jit(solution)/shard_map/ppermute | solution.py:283
  36.1 0.2 shard_map.69
  36.3 12.8 %collective-permute-start.6 = (bf16[2,144,128]{2,1,0:T(8,128)(2,1)S(1)}, bf16[2,144,128]{2,1,0:T(8,128)(2,1)S(1)}, u32[]{:S(2)}, u32[]{:S(2)}) collective-permute-start(bf16[2,144,128]{2,1,0:T(8,128)(2,1)S(1)} %get-tuple-element.42), channel_id=1, source_target_pairs={{0,2},{1,3},{2,0},{3,1},{4,6},{5,7},{6,4},{7,5},{8,10},{9,11},{10,... | collective-permute-start | bytes 221192 | tf_op jit(solution)/shard_map/ppermute | solution.py:283
  49.1 0.0 collective-permute-start.7
  49.1 2.0 %collective-permute-done.6.refs_1_ = bf16[2,144,128]{2,1,0:T(8,128)(2,1)S(1)} collective-permute-done((bf16[2,144,128]{2,1,0:T(8,128)(2,1)S(1)}, bf16[2,144,128]{2,1,0:T(8,128)(2,1)S(1)}, u32[]{:S(2)}, u32[]{:S(2)}) %collective-permute-start.6) | collective-permute-done | bytes 73760 | tf_op jit(solution)/shard_map/ppermute | solution.py:283
  51.2 0.0 collective-permute-start.8
  51.2 1.2 %collective-permute-done.7.refs_2_ = bf16[2,144,128]{2,1,0:T(8,128)(2,1)S(1)} collective-permute-done((bf16[2,144,128]{2,1,0:T(8,128)(2,1)S(1)}, bf16[2,144,128]{2,1,0:T(8,128)(2,1)S(1)}, u32[]{:S(2)}, u32[]{:S(2)}) %collective-permute-start.7) | collective-permute-done | bytes 73760 | tf_op jit(solution)/shard_map/ppermute | solution.py:283
  52.3 2.9 %collective-permute-done.8.refs_3_ = bf16[2,144,128]{2,1,0:T(8,128)(2,1)S(1)} collective-permute-done((bf16[2,144,128]{2,1,0:T(8,128)(2,1)S(1)}, bf16[2,144,128]{2,1,0:T(8,128)(2,1)S(1)}, u32[]{:S(2)}, u32[]{:S(2)}) %collective-permute-start.8) | collective-permute-done | bytes 73760 | tf_op jit(solution)/shard_map/ppermute | solution.py:283
  55.3 0.1 collective-permute-start.9
  55.4 1.1 %shard_map.72.own_ref = f32[256,1024]{1,0:T(8,128)S(1)} custom-call(bf16[256,1024]{1,0:T(8,128)(2,1)S(1)} %get-tuple-element.29.query_0_ref.query_ref, bf16[256,1024]{1,0:T(8,128)(2,1)S(1)} %get-tuple-element.46.key_ref, bf16[256,1024]{1,0:T(8,128)(2,1)S(1)} %get-tuple-element.47.value_ref), custom_call_target="tpu_custom_call" | custom-call | tf_op jit(solution)/shard_map/pallas_call | solution.py:267
  56.4 1.1 %shard_map.75.own_ref = f32[256,1024]{1,0:T(8,128)S(1)} custom-call(bf16[256,1024]{1,0:T(8,128)(2,1)S(1)} %get-tuple-element.30.query_1_ref.query_ref, bf16[256,1024]{1,0:T(8,128)(2,1)S(1)} %get-tuple-element.48.key_ref, bf16[256,1024]{1,0:T(8,128)(2,1)S(1)} %get-tuple-element.45.value_ref), custom_call_target="tpu_custom_call" | custom-call | tf_op jit(solution)/shard_map/pallas_call | solution.py:267
  57.5 1.3 %shard_map.65.phi_ref = bf16[16,256,144]{2,1,0:T(8,128)(2,1)S(1)} custom-call(s32[2,128]{1,0:T(2,128)S(1)} %get-tuple-element.27.hash_ref, s32[2,128]{1,0:T(2,128)S(1)} %get-tuple-element.28.sign_ref, bf16[256,1024]{1,0:T(8,128)(2,1)S(1)} %get-tuple-element.29.query_0_ref.query_ref, bf16[256,1024]{1,0:T(8,128)(2,1)S(1)} %get-tuple-element.30.query_1_ref.query_ref), custom_call_target="tpu_custom_call" | custom-call | tf_op jit(solution)/shard_map/pallas_call | solution.py:267
  58.9 0.0 collective-permute-done.10.key_ref
  58.9 2.2 %shard_map.74.weight_ref = bf16[8,256,256]{2,1,0:T(8,128)(2,1)S(1)} custom-call(s32[2,128]{1,0:T(2,128)S(1)} %get-tuple-element.27.hash_ref, s32[2,128]{1,0:T(2,128)S(1)} %get-tuple-element.28.sign_ref, bf16[256,1024]{1,0:T(8,128)(2,1)S(1)} %get-tuple-element.30.query_1_ref.query_ref, bf16[256,2048]{1,0:T(8,128)(2,1)S(1)} %collective-permute-done.10.key_ref), custom_call_target="tpu_custom_call" | custom-call | tf_op jit(solution)/shard_map/pallas_call | solution.py:267
  61.1 2.2 %shard_map.71.weight_ref = bf16[8,256,256]{2,1,0:T(8,128)(2,1)S(1)} custom-call(s32[2,128]{1,0:T(2,128)S(1)} %get-tuple-element.27.hash_ref, s32[2,128]{1,0:T(2,128)S(1)} %get-tuple-element.28.sign_ref, bf16[256,1024]{1,0:T(8,128)(2,1)S(1)} %get-tuple-element.29.query_0_ref.query_ref, bf16[256,2048]{1,0:T(8,128)(2,1)S(1)} %collective-permute-done.10.key_ref), custom_call_target="tpu_custom_call" | custom-call | tf_op jit(solution)/shard_map/pallas_call | solution.py:267
  63.3 0.0 collective-permute-done.12.value_ref
  63.3 0.4 shard_map.76.near_1_ref
  63.7 0.0 copy-start
  63.7 0.0 collective-permute-done.11.value_ref
  63.7 0.5 shard_map.73.near_0_ref
  64.2 0.0 collective-permute-done.9.theirs_ref
  64.2 0.2 copy-done
  64.4 1.6 %shard_map.77 = bf16[256,2048]{1,0:T(8,128)(2,1)} custom-call(bf16[16,256,144]{2,1,0:T(8,128)(2,1)S(1)} %shard_map.65.phi_ref, bf16[4,2,144,128]{3,2,1,0:T(8,128)(2,1)S(1)} %collective-permute-done.9.theirs_ref, bf16[4,2,144,128]{3,2,1,0:T(8,128)(2,1)S(1)} %shard_map.70.mine_ref, f32[256,1024]{1,0:T(8,128)S(1)} %shard_map.73.near_0_ref, ...), custom_call_target="tpu_custom_call" | custom-call | tf_op jit(solution)/shard_map/pallas_call | solution.py:267
  (2 shorter events, 0.1 us)
Async XLA Ops:
  0.0 6.4 %copy-start.1 = (bf16[256,2048]{1,0:T(8,128)(2,1)S(1)}, bf16[256,2048]{1,0:T(8,128)(2,1)}, u32[]{:S(2)}) copy-start(bf16[256,2048]{1,0:T(8,128)(2,1)} %key_hbm.1) | copy-start | bytes 3145732
  5.7 3.8 %collective-permute-start = (f32[4,2,144,128]{3,2,1,0:T(8,128)S(1)}, f32[4,2,144,128]{3,2,1,0:T(8,128)S(1)}, u32[]{:S(2)}, u32[]{:S(2)}) collective-permute-start(f32[4,2,144,128]{3,2,1,0:T(8,128)S(1)} %get-tuple-element.32), channel_id=1, source_target_pairs={{0,1},{1,0},{2,3},{3,2},{4,5},{5,4},{6,7},{7,6},{8,9},{9,8},{10,11... | collective-permute-start | bytes 1769480 | tf_op jit(solution)/shard_map/ppermute | solution.py:283
  6.4 52.4 %collective-permute-start.10 = (bf16[256,2048]{1,0:T(8,128)(2,1)S(1)}, bf16[256,2048]{1,0:T(8,128)(2,1)S(1)}, u32[]{:S(2)}, u32[]{:S(2)}) collective-permute-start(bf16[256,2048]{1,0:T(8,128)(2,1)S(1)} %copy-done.1), channel_id=1, source_target_pairs={{0,1},{1,2},{2,3},{3,4},{4,5},{5,6},{6,7},{7,8},{8,9},{9,10},{10,1... | collective-permute-start | bytes 3145736 | tf_op jit(solution)/shard_map/ppermute | solution.py:278
  9.6 15.0 %collective-permute-start.1 = (bf16[2,144,128]{2,1,0:T(8,128)(2,1)S(1)}, bf16[2,144,128]{2,1,0:T(8,128)(2,1)S(1)}, u32[]{:S(2)}, u32[]{:S(2)}) collective-permute-start(bf16[2,144,128]{2,1,0:T(8,128)(2,1)S(1)} %get-tuple-element.34), channel_id=1, source_target_pairs={{0,2},{1,3},{2,0},{3,1},{4,6},{5,7},{6,4},{7,5},{8,10},{9,11},{10,... | collective-permute-start | bytes 221192 | tf_op jit(solution)/shard_map/ppermute | solution.py:283
  9.7 15.3 %collective-permute-start.2 = (bf16[2,144,128]{2,1,0:T(8,128)(2,1)S(1)}, bf16[2,144,128]{2,1,0:T(8,128)(2,1)S(1)}, u32[]{:S(2)}, u32[]{:S(2)}) collective-permute-start(bf16[2,144,128]{2,1,0:T(8,128)(2,1)S(1)} %get-tuple-element.35), channel_id=1, source_target_pairs={{0,4},{1,5},{2,6},{3,7},{4,0},{5,1},{6,2},{7,3},{8,12},{9,13},{10,... | collective-permute-start | bytes 221192 | tf_op jit(solution)/shard_map/ppermute | solution.py:283
  11.1 15.0 %collective-permute-start.3 = (bf16[2,144,128]{2,1,0:T(8,128)(2,1)S(1)}, bf16[2,144,128]{2,1,0:T(8,128)(2,1)S(1)}, u32[]{:S(2)}, u32[]{:S(2)}) collective-permute-start(bf16[2,144,128]{2,1,0:T(8,128)(2,1)S(1)} %get-tuple-element.36), channel_id=1, source_target_pairs={{0,6},{1,7},{2,4},{3,5},{4,2},{5,3},{6,0},{7,1},{8,14},{9,15},{10,... | collective-permute-start | bytes 221192 | tf_op jit(solution)/shard_map/ppermute | solution.py:283
  26.1 4.9 %collective-permute-start.4 = (bf16[2,144,128]{2,1,0:T(8,128)(2,1)S(1)}, bf16[2,144,128]{2,1,0:T(8,128)(2,1)S(1)}, u32[]{:S(2)}, u32[]{:S(2)}) collective-permute-start(bf16[2,144,128]{2,1,0:T(8,128)(2,1)S(1)} %get-tuple-element.38), channel_id=1, source_target_pairs={{0,8},{1,9},{2,10},{3,11},{4,12},{5,13},{6,14},{7,15},{8,0},{9,1},... | collective-permute-start | bytes 221192 | tf_op jit(solution)/shard_map/ppermute | solution.py:283
  27.2 36.1 %collective-permute-start.12 = (bf16[256,1024]{1,0:T(8,128)(2,1)S(1)}, bf16[256,1024]{1,0:T(8,128)(2,1)S(1)}, u32[]{:S(2)}, u32[]{:S(2)}) collective-permute-start(bf16[256,1024]{1,0:T(8,128)(2,1)S(1)} %get-tuple-element.47.value_ref), channel_id=1, source_target_pairs={{0,1},{1,2},{2,3},{3,4},{4,5},{5,6},{6,7},{7,8},{8,9},{9,10},{10,1... | collective-permute-start | bytes 1572872 | tf_op jit(solution)/shard_map/ppermute | solution.py:278
  29.1 34.6 %collective-permute-start.11 = (bf16[256,1024]{1,0:T(8,128)(2,1)S(1)}, bf16[256,1024]{1,0:T(8,128)(2,1)S(1)}, u32[]{:S(2)}, u32[]{:S(2)}) collective-permute-start(bf16[256,1024]{1,0:T(8,128)(2,1)S(1)} %get-tuple-element.45.value_ref), channel_id=1, source_target_pairs={{0,1},{1,2},{2,3},{3,4},{4,5},{5,6},{6,7},{7,8},{8,9},{9,10},{10,1... | collective-permute-start | bytes 1572872 | tf_op jit(solution)/shard_map/ppermute | solution.py:278
  31.7 4.4 %collective-permute-start.5 = (bf16[2,144,128]{2,1,0:T(8,128)(2,1)S(1)}, bf16[2,144,128]{2,1,0:T(8,128)(2,1)S(1)}, u32[]{:S(2)}, u32[]{:S(2)}) collective-permute-start(bf16[2,144,128]{2,1,0:T(8,128)(2,1)S(1)} %get-tuple-element.40), channel_id=1, source_target_pairs={{0,16},{1,17},{2,18},{3,19},{4,20},{5,21},{6,22},{7,23},{8,24},{9,... | collective-permute-start | bytes 221192 | tf_op jit(solution)/shard_map/ppermute | solution.py:283
  36.3 14.8 %collective-permute-start.6 = (bf16[2,144,128]{2,1,0:T(8,128)(2,1)S(1)}, bf16[2,144,128]{2,1,0:T(8,128)(2,1)S(1)}, u32[]{:S(2)}, u32[]{:S(2)}) collective-permute-start(bf16[2,144,128]{2,1,0:T(8,128)(2,1)S(1)} %get-tuple-element.42), channel_id=1, source_target_pairs={{0,2},{1,3},{2,0},{3,1},{4,6},{5,7},{6,4},{7,5},{8,10},{9,11},{10,... | collective-permute-start | bytes 221192 | tf_op jit(solution)/shard_map/ppermute | solution.py:283
  49.1 3.2 %collective-permute-start.7 = (bf16[2,144,128]{2,1,0:T(8,128)(2,1)S(1)}, bf16[2,144,128]{2,1,0:T(8,128)(2,1)S(1)}, u32[]{:S(2)}, u32[]{:S(2)}) collective-permute-start(bf16[2,144,128]{2,1,0:T(8,128)(2,1)S(1)} %get-tuple-element.43), channel_id=1, source_target_pairs={{0,4},{1,5},{2,6},{3,7},{4,0},{5,1},{6,2},{7,3},{8,12},{9,13},{10,... | collective-permute-start | bytes 221192 | tf_op jit(solution)/shard_map/ppermute | solution.py:283
  51.2 4.1 %collective-permute-start.8 = (bf16[2,144,128]{2,1,0:T(8,128)(2,1)S(1)}, bf16[2,144,128]{2,1,0:T(8,128)(2,1)S(1)}, u32[]{:S(2)}, u32[]{:S(2)}) collective-permute-start(bf16[2,144,128]{2,1,0:T(8,128)(2,1)S(1)} %get-tuple-element.44), channel_id=1, source_target_pairs={{0,6},{1,7},{2,4},{3,5},{4,2},{5,3},{6,0},{7,1},{8,14},{9,15},{10,... | collective-permute-start | bytes 221192 | tf_op jit(solution)/shard_map/ppermute | solution.py:283
  55.3 8.9 %collective-permute-start.9 = (bf16[4,2,144,128]{3,2,1,0:T(8,128)(2,1)S(1)}, bf16[4,2,144,128]{3,2,1,0:T(8,128)(2,1)S(1)}, u32[]{:S(2)}, u32[]{:S(2)}) collective-permute-start(bf16[4,2,144,128]{3,2,1,0:T(8,128)(2,1)S(1)} %shard_map.70.mine_ref), channel_id=1, source_target_pairs={{0,1},{1,0},{2,3},{3,2},{4,5},{5,4},{6,7},{7,6},{8,9},{9,8},{10,11... | collective-permute-start | bytes 884744 | tf_op jit(solution)/shard_map/ppermute | solution.py:283
  63.7 0.7 %copy-start = (f32[2048]{0:T(1024)S(1)}, f32[2048]{0:T(1024)}, u32[]{:S(2)}) copy-start(f32[2048]{0:T(1024)} %param.9) | copy-start | bytes 24580

commit v4 on v3

--- a/solution.py
+++ b/solution.py
@@ -17,7 +17,8 @@
 EPS = 1e-06
 CORES = 2
 PLANE = 4
-CHUNKS = 4
+RADIX = 2
+CHUNKS = 2
 BF16 = jnp.bfloat16
 F32 = jnp.float32
 VMEM_LIMIT = 12 * 1024 * 1024
@@ -59,8 +60,8 @@
     return pl.ds(pl.multiple_of(start, HD), width)
 
 
-def quartic(scores):
-    squared = scores * scores * (1.0 / HD)
+def quartic(scores, factor=1.0 / HD):
+    squared = scores * scores * factor
     return squared * squared
 
 
@@ -196,30 +197,41 @@
 
 def weights_kernel(half, hash_ref, sign_ref, query_ref, key_ref, weight_ref):
     core, _ = place()
-    even = jnp.where(core == 0, 1.0, 0.0)
-    half_width = query_ref.shape[1]
-    row = lax.broadcasted_iota(jnp.int32, (BUCKETS, HD), 0)
-    sketch = jnp.concatenate(
-        [
-            sketch_rows(row, hash_ref[level : level + 1, :], sign_ref[level : level + 1, :])
-            for level in range(2)
-        ],
-        0,
-    )
-    for head in range(half_width // HD):
-        query = query_ref[:, head_cols(head)]
-        key = key_ref[:, dynamic_cols(side_of(half) * half_width + head * HD, HD)]
-        query_both = dot_nt(sketch, query)
-        key_both = dot_nt(sketch, key)
-        query_high, query_low = split(
-            query_both[:BUCKETS] * query_both[BUCKETS:] * (even * FACTOR2)
+    width = query_ref.shape[1]
+    heads = width // HD
+
+    def key_of(head):
+        return key_ref[:, dynamic_cols(side_of(half) * width + head * HD, HD)]
+
+    @pl.when(core == 1)
+    def _():
+        for head in range(heads):
+            cols = head_cols(head)
+            weight_ref[head] = quartic(dot_nt(query_ref[:, cols], key_of(head))).astype(BF16)
+
+    @pl.when(core == 0)
+    def _():
+        live = jnp.where(lax.axis_index("seq") == 0, 0.0, 1.0)
+        row = lax.broadcasted_iota(jnp.int32, (BUCKETS, HD), 0)
+        sketch = jnp.concatenate(
+            [
+                sketch_rows(row, hash_ref[level : level + 1, :], sign_ref[level : level + 1, :])
+                for level in range(2)
+            ],
+            0,
         )
-        key_high, key_low = split(key_both[:BUCKETS] * key_both[BUCKETS:] * FACTOR2)
-        query_parts = jnp.concatenate([query_high, query_high, query_low], 0)
-        key_parts = jnp.concatenate([key_high, key_low, key_high], 0)
-        sketched = dot_tn(query_parts, key_parts)
-        weights = quartic(dot_nt(query, key)) - sketched * sketched
-        weight_ref[head] = weights.astype(BF16)
+        for head in range(heads):
+            cols = head_cols(head)
+            query, key = query_ref[:, cols], key_of(head)
+            query_both = dot_nt(sketch, query)
+            key_both = dot_nt(sketch, key)
+            query_high, query_low = split(query_both[:BUCKETS] * query_both[BUCKETS:] * (live * FACTOR2))
+            key_high, key_low = split(key_both[:BUCKETS] * key_both[BUCKETS:] * FACTOR2)
+            query_parts = jnp.concatenate([query_high, query_high, query_low], 0)
+            key_parts = jnp.concatenate([key_high, key_low, key_high], 0)
+            sketched = dot_tn(query_parts, key_parts)
+            weights = quartic(dot_nt(query, key), live / HD) - sketched * sketched
+            weight_ref[head] = weights.astype(BF16)
 
 
 def values_kernel(weight_ref, value_ref, own_ref, near_ref):
@@ -272,10 +284,10 @@
     )(*[pltpu.with_memory_space_constraint(arg, space) for arg in args])
 
 
-def from_behind(block, axis, distance):
-    devices = range(lax.axis_size(axis))
-    route = [(i - distance, i) for i in devices if i - distance in devices]
-    return lax.ppermute(block, axis, route)
+def from_behind(block, closed=False):
+    devices = lax.axis_size("seq")
+    route = [(i, (i + 1) % devices) for i in range(devices if closed else devices - 1)]
+    return lax.ppermute(block, "seq", route)
 
 
 def swap(block, mask):
@@ -298,30 +310,35 @@
     sent_ref[...] = total.astype(BF16)
 
 
-def later_half(mask):
-    return (lax.axis_index("seq") // mask) % 2
-
-
-def first_across_kernel(mask, total_ref, got_ref, earlier_ref, more_ref, sent_ref):
-    got = got_ref[...].astype(F32)
-    earlier_ref[...] = jnp.where(later_half(mask) == 1, got, 0.0)
-    total = total_ref[...] + got
+def sum_of_earlier(unit, got_refs):
+    digit = (lax.axis_index("seq") // unit) % (len(got_refs) + 1)
+    earlier = 0.0
+    for other, got_ref in enumerate(got_refs, 1):
+        ahead = (digit ^ other) < digit
+        earlier = earlier + jnp.where(ahead, got_ref[...].astype(F32), 0.0)
+    return earlier
+
+
+def across_kernel(unit, known, total_ref, *refs):
+    known_refs, got_refs, (earlier_ref, more_ref, sent_ref) = refs[:known], refs[known:-3], refs[-3:]
+    earlier = sum_of_earlier(unit, got_refs)
+    for known_ref in known_refs:
+        earlier = earlier + known_ref[...]
+    earlier_ref[...] = earlier
+    total = total_ref[...]
+    for got_ref in got_refs:
+        total = total + got_ref[...].astype(F32)
     more_ref[...] = total
     sent_ref[...] = total.astype(BF16)
 
 
-def next_across_kernel(mask, earlier_before_ref, total_ref, got_ref, earlier_ref, more_ref, sent_ref):
-    got = got_ref[...].astype(F32)
-    earlier_ref[...] = earlier_before_ref[...] + jnp.where(later_half(mask) == 1, got, 0.0)
-    total = total_ref[...] + got
-    more_ref[...] = total
-    sent_ref[...] = total.astype(BF16)
-
-
-def prefix_kernel(mask, earlier_ref, got_ref, *refs):
+def prefix_kernel(unit, known, *refs):
     _, chip = place()
-    share_refs, prefix_refs = refs[:PLANE], refs[PLANE:]
-    earlier = earlier_ref[...] + jnp.where(later_half(mask) == 1, got_ref[...].astype(F32), 0.0)
+    known_refs, share_refs = refs[:known], refs[known : known + PLANE]
+    got_refs, prefix_refs = refs[known + PLANE : -PLANE], refs[-PLANE:]
+    earlier = sum_of_earlier(unit, got_refs)
+    for known_ref in known_refs:
+        earlier = earlier + known_ref[...]
     shares = [share_ref[...].astype(F32) for share_ref in share_refs]
     for piece, prefix_ref in enumerate(prefix_refs):
         prefix = earlier
@@ -347,21 +364,22 @@
     )
     shares = [own] + [swap(block, CORES * m) for m, block in enumerate(sent, 1)]
     total, block = kernel_call(plane_sum_kernel, (wide, narrow), *shares)
-    mask = CORES * PLANE
-    got = swap(block, mask)
-    earlier, total, block = kernel_call(
-        functools.partial(first_across_kernel, mask), (wide, wide, narrow), total, got
-    )
-    mask *= 2
-    got = swap(block, mask)
-    while mask * 2 < devices:
+    unit, known = CORES * PLANE, ()
+    while True:
+        radix = min(RADIX, devices // unit)
+        got = [swap(block, unit * m) for m in range(1, radix)]
+        if unit * radix >= devices:
+            break
         earlier, total, block = kernel_call(
-            functools.partial(next_across_kernel, mask), (wide, wide, narrow), earlier, total, got
+            functools.partial(across_kernel, unit, len(known)),
+            (wide, wide, narrow),
+            total,
+            *known,
+            *got,
         )
-        mask *= 2
-        got = swap(block, mask)
+        unit, known = unit * radix, (earlier,)
     prefixes = kernel_call(
-        functools.partial(prefix_kernel, mask), (narrow,) * PLANE, earlier, got, *shares
+        functools.partial(prefix_kernel, unit, len(known)), (narrow,) * PLANE, *known, *shares, *got
     )
     mine = kernel_call(
         stack_kernel,
@@ -381,7 +399,6 @@
     half_near = pltpu.VMEM((rows, width // 2), F32)
     id_shape = pltpu.VMEM(hash_ids.shape, hash_ids.dtype)
 
-    key_prev = from_behind(keys, "seq", 1)
     send, keep, hash_near, sign_near, query_0, query_1, key_0, key_1, value_0, value_1 = kernel_call(
         state_kernel,
         (half_state, half_state, id_shape, id_shape) + (half_rows,) * 6,
@@ -394,8 +411,9 @@
         in_specs=[IN_HBM] * 5,
         scratch_shapes=[pltpu.SemaphoreType.DMA((4 + 4 * CHUNKS,))],
     )
-    value_prev_1 = from_behind(value_0, "seq", 1)
-    value_prev_0 = from_behind(value_1, "seq", 1)
+    key_prev = from_behind(keys, closed=True)
+    value_prev_1 = from_behind(value_0)
+    value_prev_0 = from_behind(value_1)
     mine, theirs = earlier_chips(keep, send)
     phi = kernel_call(
         query_kernel,

time: 66.2 us -> 63.5 us (0.959)
  the two profiles are of different devices: /device:TPU:29 before, /device:TPU:16 now
where the time goes in v4:
time: 63.5 us; the launch traced here: 62.5 us
  waiting for transfers between devices  23.9 us (38%)
  starting transfers between devices  21.9 us (34%)
  Pallas kernels  16.3 us (26%)
    ppermute x10, waiting for transfers between devices, swap(): return lax.ppermute(block, 'seq', route)  23.9 us
    ppermute x10, starting transfers between devices, swap(): return lax.ppermute(block, 'seq', route)  17.6 us
    pallas_call x14, Pallas kernels, kernel_call(): pl.pallas_call(body, out_shape=out_shape, compiler_params=pltpu.CompilerP...  16.3 us
    ppermute x3, starting transfers between devices, from_behind(): return lax.ppermute(block, 'seq', route)  4.32 us
  transfers between devices with their start and end apart: 13, of which 8 were waited for; matrix products, arithmetic and copies ran while one was open for 0% of the time, Pallas kernels for 16%

profile of v4, /device:TPU:16, one launch (start us, length us, event | category | flops | bytes accessed | tf_op | source)
XLA Modules:
  0.0 62.5 jit_solution(574661865307475544)
XLA Ops:
  0.0 0.0 copy-start.1
  0.0 4.9 %shard_map.64 = (f32[4,2,144,128]{3,2,1,0:T(8,128)S(1)}, f32[4,2,144,128]{3,2,1,0:T(8,128)S(1)}, s32[2,128]{1,0:T(2,128)S(1)}, s32[2,128]{1,0:T(2,128)S(1)}, bf1...) custom-call(s32[2,128]{1,0:T(2,128)} %hash_hbm.1, ...), custom_call_target="tpu_custom_call" | custom-call | tf_op jit(solution)/shard_map/pallas_call | solution.py:279
  5.0 0.1 collective-permute-start
  5.0 0.0 copy-done.1
  5.0 0.5 collective-permute-start.10
  5.5 1.5 %collective-permute-done.got_ref = f32[4,2,144,128]{3,2,1,0:T(8,128)S(1)} collective-permute-done((f32[4,2,144,128]{3,2,1,0:T(8,128)S(1)}, f32[4,2,144,128]{3,2,1,0:T(8,128)S(1)}, u32[]{:S(2)}, u32[]{:S(2)}) %collective-permute-start) | collective-permute-done | bytes 589856 | tf_op jit(solution)/shard_map/ppermute | solution.py:295
  7.0 0.1 shard_map.66
  7.1 1.6 %collective-permute-start.1 = (bf16[2,144,128]{2,1,0:T(8,128)(2,1)S(1)}, bf16[2,144,128]{2,1,0:T(8,128)(2,1)S(1)}, u32[]{:S(2)}, u32[]{:S(2)}) collective-permute-start(bf16[2,144,128]{2,1,0:T(8,128)(2,1)S(1)} %get-tuple-element.34), channel_id=1, source_target_pairs={{0,2},{1,3},{2,0},{3,1},{4,6},{5,7},{6,4},{7,5},{8,10},{9,11},{10,... | collective-permute-start | bytes 221192 | tf_op jit(solution)/shard_map/ppermute | solution.py:295
  8.7 1.5 %collective-permute-start.2 = (bf16[2,144,128]{2,1,0:T(8,128)(2,1)S(1)}, bf16[2,144,128]{2,1,0:T(8,128)(2,1)S(1)}, u32[]{:S(2)}, u32[]{:S(2)}) collective-permute-start(bf16[2,144,128]{2,1,0:T(8,128)(2,1)S(1)} %get-tuple-element.35), channel_id=1, source_target_pairs={{0,4},{1,5},{2,6},{3,7},{4,0},{5,1},{6,2},{7,3},{8,12},{9,13},{10,... | collective-permute-start | bytes 221192 | tf_op jit(solution)/shard_map/ppermute | solution.py:295
  10.2 0.5 collective-permute-start.3
  10.7 1.7 %collective-permute-done.1.refs_0_.refs_2_ = bf16[2,144,128]{2,1,0:T(8,128)(2,1)S(1)} collective-permute-done((bf16[2,144,128]{2,1,0:T(8,128)(2,1)S(1)}, bf16[2,144,128]{2,1,0:T(8,128)(2,1)S(1)}, u32[]{:S(2)}, u32[]{:S(2)}) %collective-permute-start.1) | collective-permute-done | bytes 73760 | tf_op jit(solution)/shard_map/ppermute | solution.py:295
  12.3 10.5 %collective-permute-done.2.refs_1_.refs_3_ = bf16[2,144,128]{2,1,0:T(8,128)(2,1)S(1)} collective-permute-done((bf16[2,144,128]{2,1,0:T(8,128)(2,1)S(1)}, bf16[2,144,128]{2,1,0:T(8,128)(2,1)S(1)}, u32[]{:S(2)}, u32[]{:S(2)}) %collective-permute-start.2) | collective-permute-done | bytes 73760 | tf_op jit(solution)/shard_map/ppermute | solution.py:295
  22.8 1.5 %collective-permute-done.3.refs_2_.refs_4_ = bf16[2,144,128]{2,1,0:T(8,128)(2,1)S(1)} collective-permute-done((bf16[2,144,128]{2,1,0:T(8,128)(2,1)S(1)}, bf16[2,144,128]{2,1,0:T(8,128)(2,1)S(1)}, u32[]{:S(2)}, u32[]{:S(2)}) %collective-permute-start.3) | collective-permute-done | bytes 73760 | tf_op jit(solution)/shard_map/ppermute | solution.py:295
  24.3 1.6 %collective-permute-start.4 = (bf16[2,144,128]{2,1,0:T(8,128)(2,1)S(1)}, bf16[2,144,128]{2,1,0:T(8,128)(2,1)S(1)}, u32[]{:S(2)}, u32[]{:S(2)}) collective-permute-start(bf16[2,144,128]{2,1,0:T(8,128)(2,1)S(1)} %get-tuple-element.38), channel_id=1, source_target_pairs={{0,8},{1,9},{2,10},{3,11},{4,12},{5,13},{6,14},{7,15},{8,0},{9,1},... | collective-permute-start | bytes 221192 | tf_op jit(solution)/shard_map/ppermute | solution.py:295
  26.0 1.9 %collective-permute-start.12 = (bf16[256,1024]{1,0:T(8,128)(2,1)S(1)}, bf16[256,1024]{1,0:T(8,128)(2,1)S(1)}, u32[]{:S(2)}, u32[]{:S(2)}) collective-permute-start(bf16[256,1024]{1,0:T(8,128)(2,1)S(1)} %get-tuple-element.47.value_ref), channel_id=1, source_target_pairs={{0,1},{1,2},{2,3},{3,4},{4,5},{5,6},{6,7},{7,8},{8,9},{9,10},{10,1... | collective-permute-start | bytes 1572872 | tf_op jit(solution)/shard_map/ppermute | solution.py:290
  27.9 1.9 %collective-permute-start.11 = (bf16[256,1024]{1,0:T(8,128)(2,1)S(1)}, bf16[256,1024]{1,0:T(8,128)(2,1)S(1)}, u32[]{:S(2)}, u32[]{:S(2)}) collective-permute-start(bf16[256,1024]{1,0:T(8,128)(2,1)S(1)} %get-tuple-element.45.value_ref), channel_id=1, source_target_pairs={{0,1},{1,2},{2,3},{3,4},{4,5},{5,6},{6,7},{7,8},{8,9},{9,10},{10,1... | collective-permute-start | bytes 1572872 | tf_op jit(solution)/shard_map/ppermute | solution.py:290
  29.8 0.0 collective-permute-done.4.refs_0_
  29.8 0.7 %shard_map.68 = (f32[2,144,128]{2,1,0:T(8,128)S(1)}, f32[2,144,128]{2,1,0:T(8,128)}, bf16[2,144,128]{2,1,0:T(8,128)(2,1)S(1)}) custom-call(f32[2,144,128]{2,1,0:T(8,128)S(1)} %get-tuple-element.37.total_ref, bf16[2,144,128]{2,1,0:T(8,128)(2,1)S(1)} %collective-permute-done.4.refs_0_), custom_call_target="tpu_custom_call" | custom-call | tf_op jit(solution)/shard_map/pallas_call | solution.py:279
  30.5 0.5 collective-permute-start.5
  31.1 4.9 %collective-permute-done.5.refs_5_ = bf16[2,144,128]{2,1,0:T(8,128)(2,1)S(1)} collective-permute-done((bf16[2,144,128]{2,1,0:T(8,128)(2,1)S(1)}, bf16[2,144,128]{2,1,0:T(8,128)(2,1)S(1)}, u32[]{:S(2)}, u32[]{:S(2)}) %collective-permute-start.5) | collective-permute-done | bytes 73760 | tf_op jit(solution)/shard_map/ppermute | solution.py:295
  36.0 0.2 shard_map.69
  36.1 2.3 %collective-permute-start.6 = (bf16[2,144,128]{2,1,0:T(8,128)(2,1)S(1)}, bf16[2,144,128]{2,1,0:T(8,128)(2,1)S(1)}, u32[]{:S(2)}, u32[]{:S(2)}) collective-permute-start(bf16[2,144,128]{2,1,0:T(8,128)(2,1)S(1)} %get-tuple-element.42), channel_id=1, source_target_pairs={{0,2},{1,3},{2,0},{3,1},{4,6},{5,7},{6,4},{7,5},{8,10},{9,11},{10,... | collective-permute-start | bytes 221192 | tf_op jit(solution)/shard_map/ppermute | solution.py:295
  38.4 1.9 %collective-permute-start.7 = (bf16[2,144,128]{2,1,0:T(8,128)(2,1)S(1)}, bf16[2,144,128]{2,1,0:T(8,128)(2,1)S(1)}, u32[]{:S(2)}, u32[]{:S(2)}) collective-permute-start(bf16[2,144,128]{2,1,0:T(8,128)(2,1)S(1)} %get-tuple-element.43), channel_id=1, source_target_pairs={{0,4},{1,5},{2,6},{3,7},{4,0},{5,1},{6,2},{7,3},{8,12},{9,13},{10,... | collective-permute-start | bytes 221192 | tf_op jit(solution)/shard_map/ppermute | solution.py:295
  40.3 1.2 %collective-permute-done.6.refs_1_ = bf16[2,144,128]{2,1,0:T(8,128)(2,1)S(1)} collective-permute-done((bf16[2,144,128]{2,1,0:T(8,128)(2,1)S(1)}, bf16[2,144,128]{2,1,0:T(8,128)(2,1)S(1)}, u32[]{:S(2)}, u32[]{:S(2)}) %collective-permute-start.6) | collective-permute-done | bytes 73760 | tf_op jit(solution)/shard_map/ppermute | solution.py:295
  41.5 3.6 %collective-permute-start.8 = (bf16[2,144,128]{2,1,0:T(8,128)(2,1)S(1)}, bf16[2,144,128]{2,1,0:T(8,128)(2,1)S(1)}, u32[]{:S(2)}, u32[]{:S(2)}) collective-permute-start(bf16[2,144,128]{2,1,0:T(8,128)(2,1)S(1)} %get-tuple-element.44), channel_id=1, source_target_pairs={{0,6},{1,7},{2,4},{3,5},{4,2},{5,3},{6,0},{7,1},{8,14},{9,15},{10,... | collective-permute-start | bytes 221192 | tf_op jit(solution)/shard_map/ppermute | solution.py:295
  45.1 0.5 collective-permute-done.7.refs_2_
  45.7 2.1 %collective-permute-done.8.refs_3_ = bf16[2,144,128]{2,1,0:T(8,128)(2,1)S(1)} collective-permute-done((bf16[2,144,128]{2,1,0:T(8,128)(2,1)S(1)}, bf16[2,144,128]{2,1,0:T(8,128)(2,1)S(1)}, u32[]{:S(2)}, u32[]{:S(2)}) %collective-permute-start.8) | collective-permute-done | bytes 73760 | tf_op jit(solution)/shard_map/ppermute | solution.py:295
  47.8 4.0 %collective-permute-start.9 = (bf16[4,2,144,128]{3,2,1,0:T(8,128)(2,1)S(1)}, bf16[4,2,144,128]{3,2,1,0:T(8,128)(2,1)S(1)}, u32[]{:S(2)}, u32[]{:S(2)}) collective-permute-start(bf16[4,2,144,128]{3,2,1,0:T(8,128)(2,1)S(1)} %shard_map.70.mine_ref), channel_id=1, source_target_pairs={{0,1},{1,0},{2,3},{3,2},{4,5},{5,4},{6,7},{7,6},{8,9},{9,8},{10,11... | collective-permute-start | bytes 884744 | tf_op jit(solution)/shard_map/ppermute | solution.py:295
  51.8 1.1 %shard_map.72.own_ref = f32[256,1024]{1,0:T(8,128)S(1)} custom-call(bf16[256,1024]{1,0:T(8,128)(2,1)S(1)} %get-tuple-element.29.query_0_ref.query_ref, bf16[256,1024]{1,0:T(8,128)(2,1)S(1)} %get-tuple-element.46.key_ref, bf16[256,1024]{1,0:T(8,128)(2,1)S(1)} %get-tuple-element.47.value_ref), custom_call_target="tpu_custom_call" | custom-call | tf_op jit(solution)/shard_map/pallas_call | solution.py:279
  52.9 1.1 %shard_map.75.own_ref = f32[256,1024]{1,0:T(8,128)S(1)} custom-call(bf16[256,1024]{1,0:T(8,128)(2,1)S(1)} %get-tuple-element.30.query_1_ref.query_ref, bf16[256,1024]{1,0:T(8,128)(2,1)S(1)} %get-tuple-element.48.key_ref, bf16[256,1024]{1,0:T(8,128)(2,1)S(1)} %get-tuple-element.45.value_ref), custom_call_target="tpu_custom_call" | custom-call | tf_op jit(solution)/shard_map/pallas_call | solution.py:279
  54.0 1.3 %shard_map.65.phi_ref = bf16[16,256,144]{2,1,0:T(8,128)(2,1)S(1)} custom-call(s32[2,128]{1,0:T(2,128)S(1)} %get-tuple-element.27.hash_ref, s32[2,128]{1,0:T(2,128)S(1)} %get-tuple-element.28.sign_ref, bf16[256,1024]{1,0:T(8,128)(2,1)S(1)} %get-tuple-element.29.query_0_ref.query_ref, bf16[256,1024]{1,0:T(8,128)(2,1)S(1)} %get-tuple-element.30.query_1_ref.query_ref), custom_call_target="tpu_custom_call" | custom-call | tf_op jit(solution)/shard_map/pallas_call | solution.py:279
  55.3 0.0 collective-permute-done.10.key_ref
  55.3 2.2 %shard_map.74.weight_ref = bf16[8,256,256]{2,1,0:T(8,128)(2,1)S(1)} custom-call(s32[2,128]{1,0:T(2,128)S(1)} %get-tuple-element.27.hash_ref, s32[2,128]{1,0:T(2,128)S(1)} %get-tuple-element.28.sign_ref, bf16[256,1024]{1,0:T(8,128)(2,1)S(1)} %get-tuple-element.30.query_1_ref.query_ref, bf16[256,2048]{1,0:T(8,128)(2,1)S(1)} %collective-permute-done.10.key_ref), custom_call_target="tpu_custom_call" | custom-call | tf_op jit(solution)/shard_map/pallas_call | solution.py:279
  57.6 2.2 %shard_map.71.weight_ref = bf16[8,256,256]{2,1,0:T(8,128)(2,1)S(1)} custom-call(s32[2,128]{1,0:T(2,128)S(1)} %get-tuple-element.27.hash_ref, s32[2,128]{1,0:T(2,128)S(1)} %get-tuple-element.28.sign_ref, bf16[256,1024]{1,0:T(8,128)(2,1)S(1)} %get-tuple-element.29.query_0_ref.query_ref, bf16[256,2048]{1,0:T(8,128)(2,1)S(1)} %collective-permute-done.10.key_ref), custom_call_target="tpu_custom_call" | custom-call | tf_op jit(solution)/shard_map/pallas_call | solution.py:279
  59.8 0.0 collective-permute-done.12.value_ref
  59.8 0.4 shard_map.76.near_1_ref
  60.2 0.0 copy-start
  60.2 0.0 collective-permute-done.11.value_ref
  60.2 0.5 shard_map.73.near_0_ref
  60.7 0.0 collective-permute-done.9.theirs_ref
  60.7 0.2 copy-done
  60.9 1.6 %shard_map.77 = bf16[256,2048]{1,0:T(8,128)(2,1)} custom-call(bf16[16,256,144]{2,1,0:T(8,128)(2,1)S(1)} %shard_map.65.phi_ref, bf16[4,2,144,128]{3,2,1,0:T(8,128)(2,1)S(1)} %collective-permute-done.9.theirs_ref, bf16[4,2,144,128]{3,2,1,0:T(8,128)(2,1)S(1)} %shard_map.70.mine_ref, f32[256,1024]{1,0:T(8,128)S(1)} %shard_map.73.near_0_ref, ...), custom_call_target="tpu_custom_call" | custom-call | tf_op jit(solution)/shard_map/pallas_call | solution.py:279
  (2 shorter events, 0.1 us)
Async XLA Ops:
  0.0 5.0 %copy-start.1 = (bf16[256,2048]{1,0:T(8,128)(2,1)S(1)}, bf16[256,2048]{1,0:T(8,128)(2,1)}, u32[]{:S(2)}) copy-start(bf16[256,2048]{1,0:T(8,128)(2,1)} %key_hbm.1) | copy-start | bytes 3145732
  5.0 2.1 %collective-permute-start = (f32[4,2,144,128]{3,2,1,0:T(8,128)S(1)}, f32[4,2,144,128]{3,2,1,0:T(8,128)S(1)}, u32[]{:S(2)}, u32[]{:S(2)}) collective-permute-start(f32[4,2,144,128]{3,2,1,0:T(8,128)S(1)} %get-tuple-element.32), channel_id=1, source_target_pairs={{0,1},{1,0},{2,3},{3,2},{4,5},{5,4},{6,7},{7,6},{8,9},{9,8},{10,11... | collective-permute-start | bytes 1769480 | tf_op jit(solution)/shard_map/ppermute | solution.py:295
  5.0 50.3 %collective-permute-start.10 = (bf16[256,2048]{1,0:T(8,128)(2,1)S(1)}, bf16[256,2048]{1,0:T(8,128)(2,1)S(1)}, u32[]{:S(2)}, u32[]{:S(2)}) collective-permute-start(bf16[256,2048]{1,0:T(8,128)(2,1)S(1)} %copy-done.1), channel_id=1, source_target_pairs={{0,1},{1,2},{2,3},{3,4},{4,5},{5,6},{6,7},{7,8},{8,9},{9,10},{10,1... | collective-permute-start | bytes 3145736 | tf_op jit(solution)/shard_map/ppermute | solution.py:290
  7.1 5.2 %collective-permute-start.1 = (bf16[2,144,128]{2,1,0:T(8,128)(2,1)S(1)}, bf16[2,144,128]{2,1,0:T(8,128)(2,1)S(1)}, u32[]{:S(2)}, u32[]{:S(2)}) collective-permute-start(bf16[2,144,128]{2,1,0:T(8,128)(2,1)S(1)} %get-tuple-element.34), channel_id=1, source_target_pairs={{0,2},{1,3},{2,0},{3,1},{4,6},{5,7},{6,4},{7,5},{8,10},{9,11},{10,... | collective-permute-start | bytes 221192 | tf_op jit(solution)/shard_map/ppermute | solution.py:295
  8.7 14.1 %collective-permute-start.2 = (bf16[2,144,128]{2,1,0:T(8,128)(2,1)S(1)}, bf16[2,144,128]{2,1,0:T(8,128)(2,1)S(1)}, u32[]{:S(2)}, u32[]{:S(2)}) collective-permute-start(bf16[2,144,128]{2,1,0:T(8,128)(2,1)S(1)} %get-tuple-element.35), channel_id=1, source_target_pairs={{0,4},{1,5},{2,6},{3,7},{4,0},{5,1},{6,2},{7,3},{8,12},{9,13},{10,... | collective-permute-start | bytes 221192 | tf_op jit(solution)/shard_map/ppermute | solution.py:295
  10.2 14.1 %collective-permute-start.3 = (bf16[2,144,128]{2,1,0:T(8,128)(2,1)S(1)}, bf16[2,144,128]{2,1,0:T(8,128)(2,1)S(1)}, u32[]{:S(2)}, u32[]{:S(2)}) collective-permute-start(bf16[2,144,128]{2,1,0:T(8,128)(2,1)S(1)} %get-tuple-element.36), channel_id=1, source_target_pairs={{0,6},{1,7},{2,4},{3,5},{4,2},{5,3},{6,0},{7,1},{8,14},{9,15},{10,... | collective-permute-start | bytes 221192 | tf_op jit(solution)/shard_map/ppermute | solution.py:295
  24.3 5.5 %collective-permute-start.4 = (bf16[2,144,128]{2,1,0:T(8,128)(2,1)S(1)}, bf16[2,144,128]{2,1,0:T(8,128)(2,1)S(1)}, u32[]{:S(2)}, u32[]{:S(2)}) collective-permute-start(bf16[2,144,128]{2,1,0:T(8,128)(2,1)S(1)} %get-tuple-element.38), channel_id=1, source_target_pairs={{0,8},{1,9},{2,10},{3,11},{4,12},{5,13},{6,14},{7,15},{8,0},{9,1},... | collective-permute-start | bytes 221192 | tf_op jit(solution)/shard_map/ppermute | solution.py:295
  26.0 33.8 %collective-permute-start.12 = (bf16[256,1024]{1,0:T(8,128)(2,1)S(1)}, bf16[256,1024]{1,0:T(8,128)(2,1)S(1)}, u32[]{:S(2)}, u32[]{:S(2)}) collective-permute-start(bf16[256,1024]{1,0:T(8,128)(2,1)S(1)} %get-tuple-element.47.value_ref), channel_id=1, source_target_pairs={{0,1},{1,2},{2,3},{3,4},{4,5},{5,6},{6,7},{7,8},{8,9},{9,10},{10,1... | collective-permute-start | bytes 1572872 | tf_op jit(solution)/shard_map/ppermute | solution.py:290
  27.9 32.3 %collective-permute-start.11 = (bf16[256,1024]{1,0:T(8,128)(2,1)S(1)}, bf16[256,1024]{1,0:T(8,128)(2,1)S(1)}, u32[]{:S(2)}, u32[]{:S(2)}) collective-permute-start(bf16[256,1024]{1,0:T(8,128)(2,1)S(1)} %get-tuple-element.45.value_ref), channel_id=1, source_target_pairs={{0,1},{1,2},{2,3},{3,4},{4,5},{5,6},{6,7},{7,8},{8,9},{9,10},{10,1... | collective-permute-start | bytes 1572872 | tf_op jit(solution)/shard_map/ppermute | solution.py:290
  30.5 5.4 %collective-permute-start.5 = (bf16[2,144,128]{2,1,0:T(8,128)(2,1)S(1)}, bf16[2,144,128]{2,1,0:T(8,128)(2,1)S(1)}, u32[]{:S(2)}, u32[]{:S(2)}) collective-permute-start(bf16[2,144,128]{2,1,0:T(8,128)(2,1)S(1)} %get-tuple-element.40), channel_id=1, source_target_pairs={{0,16},{1,17},{2,18},{3,19},{4,20},{5,21},{6,22},{7,23},{8,24},{9,... | collective-permute-start | bytes 221192 | tf_op jit(solution)/shard_map/ppermute | solution.py:295
  36.1 5.4 %collective-permute-start.6 = (bf16[2,144,128]{2,1,0:T(8,128)(2,1)S(1)}, bf16[2,144,128]{2,1,0:T(8,128)(2,1)S(1)}, u32[]{:S(2)}, u32[]{:S(2)}) collective-permute-start(bf16[2,144,128]{2,1,0:T(8,128)(2,1)S(1)} %get-tuple-element.42), channel_id=1, source_target_pairs={{0,2},{1,3},{2,0},{3,1},{4,6},{5,7},{6,4},{7,5},{8,10},{9,11},{10,... | collective-permute-start | bytes 221192 | tf_op jit(solution)/shard_map/ppermute | solution.py:295
  38.4 7.3 %collective-permute-start.7 = (bf16[2,144,128]{2,1,0:T(8,128)(2,1)S(1)}, bf16[2,144,128]{2,1,0:T(8,128)(2,1)S(1)}, u32[]{:S(2)}, u32[]{:S(2)}) collective-permute-start(bf16[2,144,128]{2,1,0:T(8,128)(2,1)S(1)} %get-tuple-element.43), channel_id=1, source_target_pairs={{0,4},{1,5},{2,6},{3,7},{4,0},{5,1},{6,2},{7,3},{8,12},{9,13},{10,... | collective-permute-start | bytes 221192 | tf_op jit(solution)/shard_map/ppermute | solution.py:295
  41.5 6.3 %collective-permute-start.8 = (bf16[2,144,128]{2,1,0:T(8,128)(2,1)S(1)}, bf16[2,144,128]{2,1,0:T(8,128)(2,1)S(1)}, u32[]{:S(2)}, u32[]{:S(2)}) collective-permute-start(bf16[2,144,128]{2,1,0:T(8,128)(2,1)S(1)} %get-tuple-element.44), channel_id=1, source_target_pairs={{0,6},{1,7},{2,4},{3,5},{4,2},{5,3},{6,0},{7,1},{8,14},{9,15},{10,... | collective-permute-start | bytes 221192 | tf_op jit(solution)/shard_map/ppermute | solution.py:295
  47.8 12.9 %collective-permute-start.9 = (bf16[4,2,144,128]{3,2,1,0:T(8,128)(2,1)S(1)}, bf16[4,2,144,128]{3,2,1,0:T(8,128)(2,1)S(1)}, u32[]{:S(2)}, u32[]{:S(2)}) collective-permute-start(bf16[4,2,144,128]{3,2,1,0:T(8,128)(2,1)S(1)} %shard_map.70.mine_ref), channel_id=1, source_target_pairs={{0,1},{1,0},{2,3},{3,2},{4,5},{5,4},{6,7},{7,6},{8,9},{9,8},{10,11... | collective-permute-start | bytes 884744 | tf_op jit(solution)/shard_map/ppermute | solution.py:295
  60.2 0.7 %copy-start = (f32[2048]{0:T(1024)S(1)}, f32[2048]{0:T(1024)}, u32[]{:S(2)}) copy-start(f32[2048]{0:T(1024)} %param.9) | copy-start | bytes 24580

commit v5 on v4

--- a/solution.py
+++ b/solution.py
@@ -17,8 +17,7 @@
 EPS = 1e-06
 CORES = 2
 PLANE = 4
-RADIX = 2
-CHUNKS = 2
+RADIX = 4
 BF16 = jnp.bfloat16
 F32 = jnp.float32
 VMEM_LIMIT = 12 * 1024 * 1024
@@ -87,27 +86,27 @@
     per_piece = keep_ref.shape[1]
     half_width = key_0_ref.shape[1]
     half_heads = half_width // HD
-    chunk_heads = max(half_heads // CHUNKS, 1)
-    chunk = chunk_heads * HD
-    chunks = half_heads // chunk_heads
+    cuts = ((0, max(half_heads // 4, 1), half_heads), (0, half_heads))
     copies = [
         pltpu.make_async_copy(hash_hbm, hash_ref, sems.at[0]),
         pltpu.make_async_copy(sign_hbm, sign_ref, sems.at[1]),
     ]
     halves = ((key_0_ref, value_0_ref), (key_1_ref, value_1_ref))
+    arrivals = {}
     for half, refs in enumerate(halves):
-        for part in range(chunks):
-            cols = dynamic_cols(side_of(half) * half_width + part * chunk, chunk)
-            inner = pl.ds(part * chunk, chunk)
+        for low, high in zip(cuts[half], cuts[half][1:]):
+            arrivals[half, low] = len(copies)
+            inner = pl.ds(low * HD, (high - low) * HD)
+            cols = dynamic_cols(side_of(half) * half_width + low * HD, (high - low) * HD)
             for hbm, ref in zip((key_hbm, value_hbm), refs):
                 copies.append(
                     pltpu.make_async_copy(hbm.at[:, cols], ref.at[:, inner], sems.at[len(copies)])
                 )
+    for copy in copies:
+        copy.start()
     for half, ref in enumerate((query_0_ref, query_1_ref)):
         cols = dynamic_cols(side_of(half) * half_width, half_width)
         copies.append(pltpu.make_async_copy(query_hbm.at[:, cols], ref, sems.at[len(copies)]))
-    for copy in copies:
-        copy.start()
     copies[0].wait()
     copies[1].wait()
     row = lax.broadcasted_iota(jnp.int32, (FEATURES, HD), 0)
@@ -122,10 +121,13 @@
     for half, (key_ref, value_ref) in enumerate(halves):
         total_ref = (send_ref, keep_ref)[half]
         for head in range(half_heads):
-            if head % chunk_heads == 0:
-                first = 2 + 2 * (half * chunks + head // chunk_heads)
+            if (half, head) in arrivals:
+                first = arrivals[half, head]
                 copies[first].wait()
                 copies[first + 1].wait()
+            if (half, head) == (0, half_heads // 2):
+                copies[-2].start()
+                copies[-1].start()
             cols = head_cols(head)
             both = dot_nt(sketch, key_ref[:, cols])
             level = both[:FEATURES] * both[FEATURES:]
@@ -302,12 +304,12 @@
 
 
 def plane_sum_kernel(own_ref, *refs):
-    share_refs, (total_ref, sent_ref) = refs[:-2], refs[-2:]
+    share_refs, total_refs = refs[: PLANE - 1], refs[PLANE - 1 :]
     total = own_ref[...]
     for share_ref in share_refs:
         total = total + share_ref[...].astype(F32)
-    total_ref[...] = total
-    sent_ref[...] = total.astype(BF16)
+    for total_ref in total_refs:
+        total_ref[...] = total.astype(total_ref.dtype)
 
 
 def sum_of_earlier(unit, got_refs):
@@ -319,8 +321,9 @@
     return earlier
 
 
-def across_kernel(unit, known, total_ref, *refs):
-    known_refs, got_refs, (earlier_ref, more_ref, sent_ref) = refs[:known], refs[known:-3], refs[-3:]
+def across_kernel(unit, known, radix, total_ref, *refs):
+    inputs = known + radix - 1
+    known_refs, got_refs, (earlier_ref, *total_refs) = refs[:known], refs[known:inputs], refs[inputs:]
     earlier = sum_of_earlier(unit, got_refs)
     for known_ref in known_refs:
         earlier = earlier + known_ref[...]
@@ -328,8 +331,8 @@
     total = total_ref[...]
     for got_ref in got_refs:
         total = total + got_ref[...].astype(F32)
-    more_ref[...] = total
-    sent_ref[...] = total.astype(BF16)
+    for more_ref in total_refs:
+        more_ref[...] = total.astype(more_ref.dtype)
 
 
 def prefix_kernel(unit, known, *refs):
@@ -363,21 +366,24 @@
         chip_sum_kernel, (wide,) + (narrow,) * (PLANE - 1), keep, swap(send, 1)
     )
     shares = [own] + [swap(block, CORES * m) for m, block in enumerate(sent, 1)]
-    total, block = kernel_call(plane_sum_kernel, (wide, narrow), *shares)
     unit, known = CORES * PLANE, ()
+    radix = min(RADIX, devices // unit)
+    shapes = (narrow,) if unit * radix >= devices else (narrow, wide)
+    block, *total = kernel_call(plane_sum_kernel, shapes, *shares)
     while True:
-        radix = min(RADIX, devices // unit)
         got = [swap(block, unit * m) for m in range(1, radix)]
         if unit * radix >= devices:
             break
-        earlier, total, block = kernel_call(
-            functools.partial(across_kernel, unit, len(known)),
-            (wide, wide, narrow),
-            total,
+        next_radix = min(RADIX, devices // (unit * radix))
+        shapes = (narrow,) if unit * radix * next_radix >= devices else (narrow, wide)
+        earlier, block, *total = kernel_call(
+            functools.partial(across_kernel, unit, len(known), radix),
+            (wide,) + shapes,
+            *total,
             *known,
             *got,
         )
-        unit, known = unit * radix, (earlier,)
+        unit, known, radix = unit * radix, (earlier,), next_radix
     prefixes = kernel_call(
         functools.partial(prefix_kernel, unit, len(known)), (narrow,) * PLANE, *known, *shares, *got
     )
@@ -409,10 +415,10 @@
         values,
         space=pltpu.HBM,
         in_specs=[IN_HBM] * 5,
-        scratch_shapes=[pltpu.SemaphoreType.DMA((4 + 4 * CHUNKS,))],
+        scratch_shapes=[pltpu.SemaphoreType.DMA((10,))],
     )
     key_prev = from_behind(keys, closed=True)
-    value_prev_1 = from_behind(value_0)
+    value_prev_1 = from_behind(value_0, closed=True)
     value_prev_0 = from_behind(value_1)
     mine, theirs = earlier_chips(keep, send)
     phi = kernel_call(

time: 63.5 us -> 64.2 us (1.011)
  the two profiles are of different devices: /device:TPU:16 before, /device:TPU:0 now
where the time goes in v5:
time: 64.2 us; the launch traced here: 64 us
  waiting for transfers between devices  26.2 us (41%)
  starting transfers between devices  21.9 us (34%)
  Pallas kernels  15.6 us (24%)
    ppermute x11, waiting for transfers between devices, swap(): return lax.ppermute(block, 'seq', route)  26.2 us
    ppermute x11, starting transfers between devices, swap(): return lax.ppermute(block, 'seq', route)  20.2 us
    pallas_call x13, Pallas kernels, kernel_call(): pl.pallas_call(body, out_shape=out_shape, compiler_params=pltpu.CompilerP...  15.6 us
    ppermute x3, starting transfers between devices, from_behind(): return lax.ppermute(block, 'seq', route)  1.73 us
  transfers between devices with their start and end apart: 14, of which 7 were waited for; matrix products, arithmetic and copies ran while one was open for 0% of the time, Pallas kernels for 14%

profile of v5, /device:TPU:0, one launch (start us, length us, event | category | flops | bytes accessed | tf_op | source)
XLA Modules:
  0.0 64.0 jit_solution(10521945476465346133)
XLA Ops:
  0.0 0.0 copy-start.1
  0.0 4.8 %shard_map.64 = (f32[4,2,144,128]{3,2,1,0:T(8,128)S(1)}, f32[4,2,144,128]{3,2,1,0:T(8,128)S(1)}, s32[2,128]{1,0:T(2,128)S(1)}, s32[2,128]{1,0:T(2,128)S(1)}, bf1...) custom-call(s32[2,128]{1,0:T(2,128)} %hash_hbm.1, ...), custom_call_target="tpu_custom_call" | custom-call | tf_op jit(solution)/shard_map/pallas_call | solution.py:281
  4.8 0.6 collective-permute-start
  5.4 0.0 copy-done.1
  5.4 0.1 collective-permute-start.11
  5.5 1.6 %collective-permute-done.got_ref = f32[4,2,144,128]{3,2,1,0:T(8,128)S(1)} collective-permute-done((f32[4,2,144,128]{3,2,1,0:T(8,128)S(1)}, f32[4,2,144,128]{3,2,1,0:T(8,128)S(1)}, u32[]{:S(2)}, u32[]{:S(2)}) %collective-permute-start) | collective-permute-done | bytes 589856 | tf_op jit(solution)/shard_map/ppermute | solution.py:297
  7.0 0.1 shard_map.66
  7.1 2.9 %collective-permute-start.1 = (bf16[2,144,128]{2,1,0:T(8,128)(2,1)S(1)}, bf16[2,144,128]{2,1,0:T(8,128)(2,1)S(1)}, u32[]{:S(2)}, u32[]{:S(2)}) collective-permute-start(bf16[2,144,128]{2,1,0:T(8,128)(2,1)S(1)} %get-tuple-element.30), channel_id=1, source_target_pairs={{0,2},{1,3},{2,0},{3,1},{4,6},{5,7},{6,4},{7,5},{8,10},{9,11},{10,... | collective-permute-start | bytes 221192 | tf_op jit(solution)/shard_map/ppermute | solution.py:297
  10.0 1.5 %collective-permute-start.2 = (bf16[2,144,128]{2,1,0:T(8,128)(2,1)S(1)}, bf16[2,144,128]{2,1,0:T(8,128)(2,1)S(1)}, u32[]{:S(2)}, u32[]{:S(2)}) collective-permute-start(bf16[2,144,128]{2,1,0:T(8,128)(2,1)S(1)} %get-tuple-element.31), channel_id=1, source_target_pairs={{0,4},{1,5},{2,6},{3,7},{4,0},{5,1},{6,2},{7,3},{8,12},{9,13},{10,... | collective-permute-start | bytes 221192 | tf_op jit(solution)/shard_map/ppermute | solution.py:297
  11.6 0.0 collective-permute-start.3
  11.6 1.6 %collective-permute-done.1.refs_0_.refs_1_ = bf16[2,144,128]{2,1,0:T(8,128)(2,1)S(1)} collective-permute-done((bf16[2,144,128]{2,1,0:T(8,128)(2,1)S(1)}, bf16[2,144,128]{2,1,0:T(8,128)(2,1)S(1)}, u32[]{:S(2)}, u32[]{:S(2)}) %collective-permute-start.1) | collective-permute-done | bytes 73760 | tf_op jit(solution)/shard_map/ppermute | solution.py:297
  13.2 13.8 %collective-permute-done.2.refs_1_.refs_2_ = bf16[2,144,128]{2,1,0:T(8,128)(2,1)S(1)} collective-permute-done((bf16[2,144,128]{2,1,0:T(8,128)(2,1)S(1)}, bf16[2,144,128]{2,1,0:T(8,128)(2,1)S(1)}, u32[]{:S(2)}, u32[]{:S(2)}) %collective-permute-start.2) | collective-permute-done | bytes 73760 | tf_op jit(solution)/shard_map/ppermute | solution.py:297
  26.9 0.0 collective-permute-done.3.refs_2_.refs_3_
  27.0 2.4 %collective-permute-start.6 = (bf16[2,144,128]{2,1,0:T(8,128)(2,1)S(1)}, bf16[2,144,128]{2,1,0:T(8,128)(2,1)S(1)}, u32[]{:S(2)}, u32[]{:S(2)}) collective-permute-start(bf16[2,144,128]{2,1,0:T(8,128)(2,1)S(1)} %shard_map.67), channel_id=1, source_target_pairs={{0,24},{1,25},{2,26},{3,27},{4,28},{5,29},{6,30},{7,31},{8,16},{9,... | collective-permute-start | bytes 221192 | tf_op jit(solution)/shard_map/ppermute | solution.py:297
  29.4 0.0 collective-permute-start.13
  29.4 1.7 %collective-permute-start.12 = (bf16[256,1024]{1,0:T(8,128)(2,1)S(1)}, bf16[256,1024]{1,0:T(8,128)(2,1)S(1)}, u32[]{:S(2)}, u32[]{:S(2)}) collective-permute-start(bf16[256,1024]{1,0:T(8,128)(2,1)S(1)} %get-tuple-element.37.value_ref), channel_id=1, source_target_pairs={{0,1},{1,2},{2,3},{3,4},{4,5},{5,6},{6,7},{7,8},{8,9},{9,10},{10,1... | collective-permute-start | bytes 1572872 | tf_op jit(solution)/shard_map/ppermute | solution.py:292
  31.0 0.1 collective-permute-start.5
  31.1 2.1 %collective-permute-done.6.refs_6_ = bf16[2,144,128]{2,1,0:T(8,128)(2,1)S(1)} collective-permute-done((bf16[2,144,128]{2,1,0:T(8,128)(2,1)S(1)}, bf16[2,144,128]{2,1,0:T(8,128)(2,1)S(1)}, u32[]{:S(2)}, u32[]{:S(2)}) %collective-permute-start.6) | collective-permute-done | bytes 73760 | tf_op jit(solution)/shard_map/ppermute | solution.py:297
  33.2 0.2 collective-permute-start.4
  33.4 3.9 %collective-permute-done.5.refs_5_ = bf16[2,144,128]{2,1,0:T(8,128)(2,1)S(1)} collective-permute-done((bf16[2,144,128]{2,1,0:T(8,128)(2,1)S(1)}, bf16[2,144,128]{2,1,0:T(8,128)(2,1)S(1)}, u32[]{:S(2)}, u32[]{:S(2)}) %collective-permute-start.5) | collective-permute-done | bytes 73760 | tf_op jit(solution)/shard_map/ppermute | solution.py:297
  37.3 0.7 %collective-permute-done.4.refs_4_ = bf16[2,144,128]{2,1,0:T(8,128)(2,1)S(1)} collective-permute-done((bf16[2,144,128]{2,1,0:T(8,128)(2,1)S(1)}, bf16[2,144,128]{2,1,0:T(8,128)(2,1)S(1)}, u32[]{:S(2)}, u32[]{:S(2)}) %collective-permute-start.4) | collective-permute-done | bytes 73760 | tf_op jit(solution)/shard_map/ppermute | solution.py:297
  38.1 0.2 shard_map.68
  38.3 1.8 %collective-permute-start.7 = (bf16[2,144,128]{2,1,0:T(8,128)(2,1)S(1)}, bf16[2,144,128]{2,1,0:T(8,128)(2,1)S(1)}, u32[]{:S(2)}, u32[]{:S(2)}) collective-permute-start(bf16[2,144,128]{2,1,0:T(8,128)(2,1)S(1)} %get-tuple-element.34), channel_id=1, source_target_pairs={{0,2},{1,3},{2,0},{3,1},{4,6},{5,7},{6,4},{7,5},{8,10},{9,11},{10,... | collective-permute-start | bytes 221192 | tf_op jit(solution)/shard_map/ppermute | solution.py:297
  40.0 6.1 %collective-permute-start.8 = (bf16[2,144,128]{2,1,0:T(8,128)(2,1)S(1)}, bf16[2,144,128]{2,1,0:T(8,128)(2,1)S(1)}, u32[]{:S(2)}, u32[]{:S(2)}) collective-permute-start(bf16[2,144,128]{2,1,0:T(8,128)(2,1)S(1)} %get-tuple-element.35), channel_id=1, source_target_pairs={{0,4},{1,5},{2,6},{3,7},{4,0},{5,1},{6,2},{7,3},{8,12},{9,13},{10,... | collective-permute-start | bytes 221192 | tf_op jit(solution)/shard_map/ppermute | solution.py:297
  46.1 0.0 collective-permute-done.7.refs_1_
  46.1 4.5 %collective-permute-start.9 = (bf16[2,144,128]{2,1,0:T(8,128)(2,1)S(1)}, bf16[2,144,128]{2,1,0:T(8,128)(2,1)S(1)}, u32[]{:S(2)}, u32[]{:S(2)}) collective-permute-start(bf16[2,144,128]{2,1,0:T(8,128)(2,1)S(1)} %get-tuple-element.36), channel_id=1, source_target_pairs={{0,6},{1,7},{2,4},{3,5},{4,2},{5,3},{6,0},{7,1},{8,14},{9,15},{10,... | collective-permute-start | bytes 221192 | tf_op jit(solution)/shard_map/ppermute | solution.py:297
  50.7 0.0 collective-permute-done.8.refs_2_
  50.7 2.6 %collective-permute-done.9.refs_3_ = bf16[2,144,128]{2,1,0:T(8,128)(2,1)S(1)} collective-permute-done((bf16[2,144,128]{2,1,0:T(8,128)(2,1)S(1)}, bf16[2,144,128]{2,1,0:T(8,128)(2,1)S(1)}, u32[]{:S(2)}, u32[]{:S(2)}) %collective-permute-start.9) | collective-permute-done | bytes 73760 | tf_op jit(solution)/shard_map/ppermute | solution.py:297
  53.3 0.1 collective-permute-start.10
  53.4 1.1 %shard_map.71.own_ref = f32[256,1024]{1,0:T(8,128)S(1)} custom-call(bf16[256,1024]{1,0:T(8,128)(2,1)S(1)} %get-tuple-element.25.query_0_ref.query_ref, bf16[256,1024]{1,0:T(8,128)(2,1)S(1)} %get-tuple-element.38.key_ref, bf16[256,1024]{1,0:T(8,128)(2,1)S(1)} %get-tuple-element.39.value_ref), custom_call_target="tpu_custom_call" | custom-call | tf_op jit(solution)/shard_map/pallas_call | solution.py:281
  54.4 1.1 %shard_map.74.own_ref = f32[256,1024]{1,0:T(8,128)S(1)} custom-call(bf16[256,1024]{1,0:T(8,128)(2,1)S(1)} %get-tuple-element.26.query_1_ref.query_ref, bf16[256,1024]{1,0:T(8,128)(2,1)S(1)} %get-tuple-element.40.key_ref, bf16[256,1024]{1,0:T(8,128)(2,1)S(1)} %get-tuple-element.37.value_ref), custom_call_target="tpu_custom_call" | custom-call | tf_op jit(solution)/shard_map/pallas_call | solution.py:281
  55.5 1.3 %shard_map.65.phi_ref = bf16[16,256,144]{2,1,0:T(8,128)(2,1)S(1)} custom-call(s32[2,128]{1,0:T(2,128)S(1)} %get-tuple-element.23.hash_ref, s32[2,128]{1,0:T(2,128)S(1)} %get-tuple-element.24.sign_ref, bf16[256,1024]{1,0:T(8,128)(2,1)S(1)} %get-tuple-element.25.query_0_ref.query_ref, bf16[256,1024]{1,0:T(8,128)(2,1)S(1)} %get-tuple-element.26.query_1_ref.query_ref), custom_call_target="tpu_custom_call" | custom-call | tf_op jit(solution)/shard_map/pallas_call | solution.py:281
  56.9 0.0 collective-permute-done.11.key_ref
  56.9 2.2 %shard_map.73.weight_ref = bf16[8,256,256]{2,1,0:T(8,128)(2,1)S(1)} custom-call(s32[2,128]{1,0:T(2,128)S(1)} %get-tuple-element.23.hash_ref, s32[2,128]{1,0:T(2,128)S(1)} %get-tuple-element.24.sign_ref, bf16[256,1024]{1,0:T(8,128)(2,1)S(1)} %get-tuple-element.26.query_1_ref.query_ref, bf16[256,2048]{1,0:T(8,128)(2,1)S(1)} %collective-permute-done.11.key_ref), custom_call_target="tpu_custom_call" | custom-call | tf_op jit(solution)/shard_map/pallas_call | solution.py:281
  59.1 2.2 %shard_map.70.weight_ref = bf16[8,256,256]{2,1,0:T(8,128)(2,1)S(1)} custom-call(s32[2,128]{1,0:T(2,128)S(1)} %get-tuple-element.23.hash_ref, s32[2,128]{1,0:T(2,128)S(1)} %get-tuple-element.24.sign_ref, bf16[256,1024]{1,0:T(8,128)(2,1)S(1)} %get-tuple-element.25.query_0_ref.query_ref, bf16[256,2048]{1,0:T(8,128)(2,1)S(1)} %collective-permute-done.11.key_ref), custom_call_target="tpu_custom_call" | custom-call | tf_op jit(solution)/shard_map/pallas_call | solution.py:281
  61.3 0.0 collective-permute-done.13.value_ref
  61.3 0.4 shard_map.75.near_1_ref
  61.7 0.0 copy-start
  61.7 0.0 collective-permute-done.12.value_ref
  61.8 0.5 shard_map.72.near_0_ref
  62.2 0.0 collective-permute-done.10.theirs_ref
  62.2 0.2 copy-done
  62.4 1.6 %shard_map.76 = bf16[256,2048]{1,0:T(8,128)(2,1)} custom-call(bf16[16,256,144]{2,1,0:T(8,128)(2,1)S(1)} %shard_map.65.phi_ref, bf16[4,2,144,128]{3,2,1,0:T(8,128)(2,1)S(1)} %collective-permute-done.10.theirs_ref, bf16[4,2,144,128]{3,2,1,0:T(8,128)(2,1)S(1)} %shard_map.69.mine_ref, f32[256,1024]{1,0:T(8,128)S(1)} %shard_map.72.near_0_ref, ...), custom_call_target="tpu_custom_call" | custom-call | tf_op jit(solution)/shard_map/pallas_call | solution.py:281
  (2 shorter events, 0.1 us)
Async XLA Ops:
  0.0 5.4 %copy-start.1 = (bf16[256,2048]{1,0:T(8,128)(2,1)S(1)}, bf16[256,2048]{1,0:T(8,128)(2,1)}, u32[]{:S(2)}) copy-start(bf16[256,2048]{1,0:T(8,128)(2,1)} %key_hbm.1) | copy-start | bytes 3145732
  4.8 2.2 %collective-permute-start = (f32[4,2,144,128]{3,2,1,0:T(8,128)S(1)}, f32[4,2,144,128]{3,2,1,0:T(8,128)S(1)}, u32[]{:S(2)}, u32[]{:S(2)}) collective-permute-start(f32[4,2,144,128]{3,2,1,0:T(8,128)S(1)} %get-tuple-element.28), channel_id=1, source_target_pairs={{0,1},{1,0},{2,3},{3,2},{4,5},{5,4},{6,7},{7,6},{8,9},{9,8},{10,11... | collective-permute-start | bytes 1769480 | tf_op jit(solution)/shard_map/ppermute | solution.py:297
  5.4 51.5 %collective-permute-start.11 = (bf16[256,2048]{1,0:T(8,128)(2,1)S(1)}, bf16[256,2048]{1,0:T(8,128)(2,1)S(1)}, u32[]{:S(2)}, u32[]{:S(2)}) collective-permute-start(bf16[256,2048]{1,0:T(8,128)(2,1)S(1)} %copy-done.1), channel_id=1, source_target_pairs={{0,1},{1,2},{2,3},{3,4},{4,5},{5,6},{6,7},{7,8},{8,9},{9,10},{10,1... | collective-permute-start | bytes 3145736 | tf_op jit(solution)/shard_map/ppermute | solution.py:292
  7.1 6.0 %collective-permute-start.1 = (bf16[2,144,128]{2,1,0:T(8,128)(2,1)S(1)}, bf16[2,144,128]{2,1,0:T(8,128)(2,1)S(1)}, u32[]{:S(2)}, u32[]{:S(2)}) collective-permute-start(bf16[2,144,128]{2,1,0:T(8,128)(2,1)S(1)} %get-tuple-element.30), channel_id=1, source_target_pairs={{0,2},{1,3},{2,0},{3,1},{4,6},{5,7},{6,4},{7,5},{8,10},{9,11},{10,... | collective-permute-start | bytes 221192 | tf_op jit(solution)/shard_map/ppermute | solution.py:297
  10.0 16.9 %collective-permute-start.2 = (bf16[2,144,128]{2,1,0:T(8,128)(2,1)S(1)}, bf16[2,144,128]{2,1,0:T(8,128)(2,1)S(1)}, u32[]{:S(2)}, u32[]{:S(2)}) collective-permute-start(bf16[2,144,128]{2,1,0:T(8,128)(2,1)S(1)} %get-tuple-element.31), channel_id=1, source_target_pairs={{0,4},{1,5},{2,6},{3,7},{4,0},{5,1},{6,2},{7,3},{8,12},{9,13},{10,... | collective-permute-start | bytes 221192 | tf_op jit(solution)/shard_map/ppermute | solution.py:297
  11.6 15.4 %collective-permute-start.3 = (bf16[2,144,128]{2,1,0:T(8,128)(2,1)S(1)}, bf16[2,144,128]{2,1,0:T(8,128)(2,1)S(1)}, u32[]{:S(2)}, u32[]{:S(2)}) collective-permute-start(bf16[2,144,128]{2,1,0:T(8,128)(2,1)S(1)} %get-tuple-element.32), channel_id=1, source_target_pairs={{0,6},{1,7},{2,4},{3,5},{4,2},{5,3},{6,0},{7,1},{8,14},{9,15},{10,... | collective-permute-start | bytes 221192 | tf_op jit(solution)/shard_map/ppermute | solution.py:297
  27.0 6.2 %collective-permute-start.6 = (bf16[2,144,128]{2,1,0:T(8,128)(2,1)S(1)}, bf16[2,144,128]{2,1,0:T(8,128)(2,1)S(1)}, u32[]{:S(2)}, u32[]{:S(2)}) collective-permute-start(bf16[2,144,128]{2,1,0:T(8,128)(2,1)S(1)} %shard_map.67), channel_id=1, source_target_pairs={{0,24},{1,25},{2,26},{3,27},{4,28},{5,29},{6,30},{7,31},{8,16},{9,... | collective-permute-start | bytes 221192 | tf_op jit(solution)/shard_map/ppermute | solution.py:297
  29.4 31.9 %collective-permute-start.13 = (bf16[256,1024]{1,0:T(8,128)(2,1)S(1)}, bf16[256,1024]{1,0:T(8,128)(2,1)S(1)}, u32[]{:S(2)}, u32[]{:S(2)}) collective-permute-start(bf16[256,1024]{1,0:T(8,128)(2,1)S(1)} %get-tuple-element.39.value_ref), channel_id=1, source_target_pairs={{0,1},{1,2},{2,3},{3,4},{4,5},{5,6},{6,7},{7,8},{8,9},{9,10},{10,1... | collective-permute-start | bytes 1572872 | tf_op jit(solution)/shard_map/ppermute | solution.py:292
  29.4 32.4 %collective-permute-start.12 = (bf16[256,1024]{1,0:T(8,128)(2,1)S(1)}, bf16[256,1024]{1,0:T(8,128)(2,1)S(1)}, u32[]{:S(2)}, u32[]{:S(2)}) collective-permute-start(bf16[256,1024]{1,0:T(8,128)(2,1)S(1)} %get-tuple-element.37.value_ref), channel_id=1, source_target_pairs={{0,1},{1,2},{2,3},{3,4},{4,5},{5,6},{6,7},{7,8},{8,9},{9,10},{10,1... | collective-permute-start | bytes 1572872 | tf_op jit(solution)/shard_map/ppermute | solution.py:292
  31.0 6.3 %collective-permute-start.5 = (bf16[2,144,128]{2,1,0:T(8,128)(2,1)S(1)}, bf16[2,144,128]{2,1,0:T(8,128)(2,1)S(1)}, u32[]{:S(2)}, u32[]{:S(2)}) collective-permute-start(bf16[2,144,128]{2,1,0:T(8,128)(2,1)S(1)} %shard_map.67), channel_id=1, source_target_pairs={{0,16},{1,17},{2,18},{3,19},{4,20},{5,21},{6,22},{7,23},{8,24},{9,... | collective-permute-start | bytes 221192 | tf_op jit(solution)/shard_map/ppermute | solution.py:297
  33.2 4.9 %collective-permute-start.4 = (bf16[2,144,128]{2,1,0:T(8,128)(2,1)S(1)}, bf16[2,144,128]{2,1,0:T(8,128)(2,1)S(1)}, u32[]{:S(2)}, u32[]{:S(2)}) collective-permute-start(bf16[2,144,128]{2,1,0:T(8,128)(2,1)S(1)} %shard_map.67), channel_id=1, source_target_pairs={{0,8},{1,9},{2,10},{3,11},{4,12},{5,13},{6,14},{7,15},{8,0},{9,1},... | collective-permute-start | bytes 221192 | tf_op jit(solution)/shard_map/ppermute | solution.py:297
  38.3 7.9 %collective-permute-start.7 = (bf16[2,144,128]{2,1,0:T(8,128)(2,1)S(1)}, bf16[2,144,128]{2,1,0:T(8,128)(2,1)S(1)}, u32[]{:S(2)}, u32[]{:S(2)}) collective-permute-start(bf16[2,144,128]{2,1,0:T(8,128)(2,1)S(1)} %get-tuple-element.34), channel_id=1, source_target_pairs={{0,2},{1,3},{2,0},{3,1},{4,6},{5,7},{6,4},{7,5},{8,10},{9,11},{10,... | collective-permute-start | bytes 221192 | tf_op jit(solution)/shard_map/ppermute | solution.py:297
  40.0 10.7 %collective-permute-start.8 = (bf16[2,144,128]{2,1,0:T(8,128)(2,1)S(1)}, bf16[2,144,128]{2,1,0:T(8,128)(2,1)S(1)}, u32[]{:S(2)}, u32[]{:S(2)}) collective-permute-start(bf16[2,144,128]{2,1,0:T(8,128)(2,1)S(1)} %get-tuple-element.35), channel_id=1, source_target_pairs={{0,4},{1,5},{2,6},{3,7},{4,0},{5,1},{6,2},{7,3},{8,12},{9,13},{10,... | collective-permute-start | bytes 221192 | tf_op jit(solution)/shard_map/ppermute | solution.py:297
  46.1 7.1 %collective-permute-start.9 = (bf16[2,144,128]{2,1,0:T(8,128)(2,1)S(1)}, bf16[2,144,128]{2,1,0:T(8,128)(2,1)S(1)}, u32[]{:S(2)}, u32[]{:S(2)}) collective-permute-start(bf16[2,144,128]{2,1,0:T(8,128)(2,1)S(1)} %get-tuple-element.36), channel_id=1, source_target_pairs={{0,6},{1,7},{2,4},{3,5},{4,2},{5,3},{6,0},{7,1},{8,14},{9,15},{10,... | collective-permute-start | bytes 221192 | tf_op jit(solution)/shard_map/ppermute | solution.py:297
  53.3 8.9 %collective-permute-start.10 = (bf16[4,2,144,128]{3,2,1,0:T(8,128)(2,1)S(1)}, bf16[4,2,144,128]{3,2,1,0:T(8,128)(2,1)S(1)}, u32[]{:S(2)}, u32[]{:S(2)}) collective-permute-start(bf16[4,2,144,128]{3,2,1,0:T(8,128)(2,1)S(1)} %shard_map.69.mine_ref), channel_id=1, source_target_pairs={{0,1},{1,0},{2,3},{3,2},{4,5},{5,4},{6,7},{7,6},{8,9},{9,8},{10,11... | collective-permute-start | bytes 884744 | tf_op jit(solution)/shard_map/ppermute | solution.py:297
  61.7 0.7 %copy-start = (f32[2048]{0:T(1024)S(1)}, f32[2048]{0:T(1024)}, u32[]{:S(2)}) copy-start(f32[2048]{0:T(1024)} %param.9) | copy-start | bytes 24580
